TPU v7x, 32 devices: a whole 2x2x4 slice. The times are simulated.
32 devices in a mesh: row: 8 (over z, y), col: 4 (over x, core).
Axes of the slice: x: 2, y: 2, z: 4, core: 2. Of those that a mesh axis runs over, the one named last changes fastest.
Arguments:
- panel_block: float32 [16384, 128], P(('row', 'col')), may hold values from -360 to 360
- trailing: float32 [16384, 2048], P('row', 'col'), may hold values from -2048 to 2048
Outputs:
- r_scaled: float32 [128, 128], replicated
- w_scaled: float32 [128, 2048], P(None, 'col')
- remainder: float32 [16384, 2048], P('row', 'col')
All inputs are finite; a program needn't handle non-finite values.
Results may differ from a plain program's by a relative error of at most 0.0003.
Values sent between devices are 32-bit elements; how exact they have to be, the bound alone decides.
No kernel may reach another device: no remote copies, remote signals or barrier semaphores. Data moves between devices by JAX's collectives and lax.ppermute only.
A program may use at most 64 MiB of HBM per device.

v0:
```python
import math

import jax
import jax.numpy as jnp
from jax import lax
from jax.sharding import PartitionSpec as P


def inner_rows(first_block, second_block):
    return jnp.einsum("rk,rc->kc", first_block, second_block, precision=lax.Precision.HIGHEST)


def upper_factor(gram):
    width = gram.shape[0]
    positions = lax.iota(jnp.int32, width)

    def column_step(index, state):
        remaining, lower = state
        picker = (positions == index).astype(jnp.float32)
        column = jnp.dot(remaining, picker, precision=lax.Precision.HIGHEST)
        pivot = jnp.sum(column * picker)
        column = jnp.where(positions >= index, column / jnp.sqrt(pivot), 0.0)
        remaining = remaining - column[:, None] * column[None, :]
        lower = lower + column[:, None] * picker[None, :]
        return (remaining, lower)

    start = (gram, jnp.zeros_like(gram))
    remaining, lower = lax.fori_loop(0, width, column_step, start)
    return lower.T


def upper_inverse(factor):
    width = factor.shape[0]
    positions = lax.iota(jnp.int32, width)

    def row_step(count, inverse):
        index = width - 1 - count
        picker = (positions == index).astype(jnp.float32)
        factor_row = jnp.dot(picker, factor, precision=lax.Precision.HIGHEST)
        pivot = jnp.sum(factor_row * picker)
        new_row = (picker - jnp.dot(factor_row, inverse, precision=lax.Precision.HIGHEST)) / pivot
        return inverse + picker[:, None] * new_row[None, :]

    return lax.fori_loop(0, width, row_step, jnp.zeros_like(factor))


def body(panel_block, trailing):
    total_rows = panel_block.shape[0] * lax.axis_size("row") * lax.axis_size("col")
    norm_scale = 1.0 / math.sqrt(total_rows)
    gathered = lax.all_gather(panel_block, "col", axis=0, tiled=True)
    cross = lax.psum(inner_rows(gathered, trailing), "row")
    local_gram = inner_rows(panel_block, panel_block)
    gram = lax.psum(local_gram, ("row", "col"))
    factor = upper_factor(gram)
    inverse = upper_inverse(factor)
    weights = jnp.dot(inverse.T, cross, precision=lax.Precision.HIGHEST)
    coeffs = jnp.dot(inverse, weights, precision=lax.Precision.HIGHEST)
    remainder = trailing - jnp.dot(gathered, coeffs, precision=lax.Precision.HIGHEST)
    return (factor * norm_scale, weights * norm_scale, remainder)


def solution(mesh):
    in_specs = (P(("row", "col"), None), P("row", "col"))
    out_specs = (P(), P(None, "col"), P("row", "col"))
    return jax.shard_map(body, mesh=mesh, in_specs=in_specs, out_specs=out_specs, check_vma=False)
```

profile of v0, /device:TPU:0, one launch (start us, length us, event | category | flops | bytes accessed | tf_op | source)
XLA Modules:
  0.0 886.0 jit_solution(7918090243251540799)
XLA Ops:
  8.0 2.3 fusion.21
  11.0 5.3 copy.6
  16.3 124.9 %all-reduce.3.cloned.1.call-done = f32[128,128]{1,0:T(8,128)} async-done(((f32[128,128]{1,0:T(8,128)}), f32[128,128]{1,0:T(8,128)}) %all-reduce.3.cloned.1.call-update) | async-done | bytes 65552 | tf_op jit(solution)/shard_map/psum | solution.py:53
  141.3 499.0 %while.32 = (s32[]{:T(128)}, f32[128,128]{1,0:T(8,128)}, f32[128,128]{1,0:T(8,128)S(1)}, s32[]{:T(128)}, s32[]{:T(128)}) while((s32[]{:T(128)}, f32[128,128]{1,0:T(8,128)}, f32[128,128]{1,0:T(8,128)S(1)}, s32[]{:T(128)}, s32[]{:T(128)}) %tuple.77), condition=%wide.region_3.4_spmd.clone.clone, body=%wide.region_1.3_spmd.clone.clone.sunk | while | flops 279682 | bytes 330859 | solution.py:28
  141.3 1.6 fusion.53
  145.2 1.6 fusion.53
  149.1 1.6 fusion.53
  153.0 1.6 fusion.53
  156.9 1.6 fusion.53
  160.8 1.6 fusion.53
  164.7 1.6 fusion.53
  168.6 1.6 fusion.53
  172.4 1.6 fusion.53
  176.3 1.6 fusion.53
  180.2 1.6 fusion.53
  184.1 1.6 fusion.53
  188.0 1.6 fusion.53
  191.9 1.6 fusion.53
  195.8 1.6 fusion.53
  199.7 1.6 fusion.53
  203.6 1.6 fusion.53
  207.5 1.6 fusion.53
  215.3 1.6 fusion.53
  219.2 1.6 fusion.53
  223.1 1.6 fusion.53
  227.0 1.6 fusion.53
  230.9 1.6 fusion.53
  640.4 5.9 fusion.22
  646.3 217.1 %while.31 = (s32[]{:T(128)}, f32[128,128]{1,0:T(8,128)S(1)}, f32[128,128]{1,0:T(8,128)S(1)}, s32[]{:T(128)}, s32[]{:T(128)}, /*index=5*/s32[]{:T(128)}) while((s32[]{:T(128)}, f32[128,128]{1,0:T(8,128)S(1)}, f32[128,128]{1,0:T(8,128)S(1)}, s32[]{:T(128)}, s32[]{:T(128)}, /*index=5*/s32[]{:T(128)}) %tuple.89), condition=%wide.region_6.0_spmd.clone, body=%wide.region_4.0_spmd.clone.sunk | while | flops 460035 | bytes 265336 | solution.py:44
  864.0 2.1 broadcast_multiply_fusion
  866.5 6.8 bitcast_subtract_fusion
  873.3 5.3 copy.7
  (1016 shorter events, 586.1 us)
Async XLA Ops:
  8.0 133.3 %all-reduce.3.cloned.1.call-start = ((), (), s32[]{:S(2)}) async-start(), calls=%async_computation | async-start | bytes 131072 | tf_op jit(solution)/shard_map/psum | solution.py:53
  10.3 630.1 %all-gather.2.cloned.1.call-start = ((), (), s32[]{:S(2)}) async-start(), calls=%async_computation.1 | async-start | bytes 1310720 | tf_op jit(solution)/shard_map/all_gather | solution.py:50
  10.9 853.1 %all-reduce.5.cloned.1.call-start = ((), (), s32[]{:S(2)}) async-start(), calls=%async_computation.2 | async-start | bytes 524288 | tf_op jit(solution)/shard_map/psum | solution.py:51
  640.4 226.1 %copy-start = (f32[2048,128]{1,0:T(8,128)S(1)}, f32[2048,128]{1,0:T(8,128)}, u32[]{:S(2)}) copy-start(f32[2048,128]{1,0:T(8,128)} %all-gather.2.cloned.1.call-done) | copy-start | bytes 3145732
Sparse Core Ops, SparseCore 0:
  15.0 126.2 all-reduce.2
Sparse Core Ops, SparseCore 1:
  12.4 19.3 all-gather.1
  646.4 72.3 all-reduce.4
where the time goes:
time: 902 us; the launch traced here: 886 us
  matrix products  425 us (47%)
  other arithmetic  215 us (24%)
  waiting for transfers between devices  126 us (14%)
  loops' own time  94.2 us (10%)
  between operations  15.5 us (2%)
  local copies, waits for them, and re-layouts  10.8 us (1%)
    dot_general x128, matrix products, column_step(): column = jnp.dot(remaining, picker, precision=lax.Precision.HIGHEST)  209 us
    add x128, other arithmetic, column_step(): lower = lower + column[:, None] * picker[None, :]  199 us
    psum x1, waiting for transfers between devices, body(): gram = lax.psum(local_gram, ('row', 'col'))  125 us
    dot_general x128, matrix products, row_step(): jnp.dot(factor_row, inverse, precision=lax.Precision.HIGHEST)  102 us
    dot_general x128, matrix products, row_step(): factor_row = jnp.dot(picker, factor, precision=lax.Precision.HIGHEST)  96.5 us
    another operation x1, loops' own time, upper_factor(): remaining, lower = lax.fori_loop(0, width, column_step, start)  89.8 us
  transfers between devices with their start and end apart: 3, of which 1 were waited for; matrix products, arithmetic and copies ran while one was open for 71% of the time, Pallas kernels for 0%

commit v1 on v0

v1 whole, which is shorter than its diff:
```python
import functools
import math

import jax
import jax.numpy as jnp
from jax import lax
from jax.experimental import pallas as pl
from jax.experimental.pallas import tpu as pltpu
from jax.sharding import PartitionSpec as P

HIGHEST = lax.Precision.HIGHEST
VMEM = pl.BlockSpec(memory_space=pltpu.VMEM)
SMEM = pl.BlockSpec(memory_space=pltpu.SMEM)
ANY = pl.BlockSpec(memory_space=pl.ANY)


def limit(mebibytes):
    return pltpu.CompilerParams(vmem_limit_bytes=mebibytes << 20)


def f32(*shape):
    return jax.ShapeDtypeStruct(shape, jnp.float32)


def split(value):
    high = value.astype(jnp.bfloat16)
    return high, (value - high.astype(jnp.float32)).astype(jnp.bfloat16)


def dot(first, second, dims, precision=None):
    return lax.dot_general(
        first, second, (dims, ((), ())), precision=precision, preferred_element_type=jnp.float32
    )


def gram_kernel(panel_ref, gram_ref):
    panel = panel_ref[...]
    gram_ref[...] = dot(panel, panel, ((0,), (0,)), HIGHEST)


def factor_kernel(gram_ref, factor_ref, inverse_ref, *, block, step):
    width = gram_ref.shape[0]
    local = lax.broadcasted_iota(jnp.int32, (step, 1), 0)
    lanes = lax.broadcasted_iota(jnp.int32, (block, width), 1)
    rows = lax.broadcasted_iota(jnp.int32, (block, width), 0)
    factor_rows, inverse_rows = [], []
    for first in range(0, width, block):
        left = gram_ref[first : first + block, :]
        right = jnp.where(lanes == rows + first, 1.0, 0.0)
        if factor_rows:
            above = jnp.concatenate(factor_rows, 0)
            both = jnp.concatenate([above, jnp.concatenate(inverse_rows, 0)], 1)
            update = dot(above[:, first : first + block], both, ((0,), (0,)), HIGHEST)
            left = left - update[:, :width]
            right = right - update[:, width:]
        left_done, right_done = [], []
        for start in range(first, first + block, step):
            columns = [
                jnp.broadcast_to(left[:, start + j : start + j + 1], left.shape) for j in range(step)
            ]
            pivots = jnp.ones((step, width), jnp.float32)
            for k in range(step):
                pivot = columns[k][k : k + 1, :]
                pivots = jnp.where(local == k, pivot, pivots)
                ratio = columns[k] * (1.0 / pivot)
                head = jnp.where(local > k, ratio[:step], 0.0)
                if ratio.shape[0] > step:
                    head = jnp.concatenate([head, ratio[step:]], 0)
                ratio = head
                for j in range(k + 1, step):
                    columns[j] = columns[j] - ratio * columns[j][k : k + 1, :]
                left = left - ratio * left[k : k + 1, :]
                right = right - ratio * right[k : k + 1, :]
            scale = lax.rsqrt(pivots)
            left_done.append(left[:step] * scale)
            right_done.append(right[:step] * scale)
            left, right = left[step:], right[step:]
        factor_rows.append(jnp.where(lanes >= rows + first, jnp.concatenate(left_done, 0), 0.0))
        inverse_rows.append(jnp.where(lanes <= rows + first, jnp.concatenate(right_done, 0), 0.0))
        factor_ref[first : first + block, :] = factor_rows[-1]
        inverse_ref[first : first + block, :] = inverse_rows[-1]


def cross_kernel(place_ref, *refs, order):
    pieces = refs[: len(order)]
    trailing_ref, mine_ref, other_ref, split_ref, buffer, total, sems = refs[len(order) :]
    piece_rows, width = pieces[0].shape
    half = width // 2

    def rows_of(index):
        return pl.ds(pl.multiple_of((place_ref[0] ^ order[index]) * piece_rows, piece_rows), piece_rows)

    copies = [
        pltpu.make_async_copy(trailing_ref.at[rows_of(i)], buffer.at[i], sems.at[i])
        for i in range(len(order))
    ]
    for copy in copies:
        copy.start()
    for i, piece in enumerate(pieces):
        high, low = split(piece[...])
        split_ref[rows_of(i), :width] = high
        split_ref[rows_of(i), width:] = low
        copies[i].wait()
        block_high, block_low = split(buffer[i])
        contract = ((0,), (0,))
        product = dot(high, block_high, contract)
        product += dot(high, block_low, contract) + dot(low, block_high, contract)
        total[...] = product if i == 0 else total[...] + product
    bit = place_ref[1]
    mine_ref[...] = total[pl.ds(pl.multiple_of(bit * half, half), half), :]
    other_ref[...] = total[pl.ds(pl.multiple_of((1 - bit) * half, half), half), :]


def final_kernel(
    place_ref, factor_ref, inverse_ref, mine_ref, other_ref, split_ref, trailing_ref,
    r_ref, w_ref, remainder_ref, buffer, result, in_sems, out_sems, *, norm_scale,
):
    blocks, block_rows, _ = buffer.shape
    width = factor_ref.shape[0]
    reads = [
        pltpu.make_async_copy(
            trailing_ref.at[pl.ds(i * block_rows, block_rows)], buffer.at[i], in_sems.at[i]
        )
        for i in range(blocks)
    ]
    for read in reads:
        read.start()
    low_first = place_ref[1] == 0
    mine, other = mine_ref[...], other_ref[...]
    cross = jnp.concatenate(
        [jnp.where(low_first, mine, other), jnp.where(low_first, other, mine)], 0
    )
    inverse = inverse_ref[...]
    weights = dot(inverse, cross, ((1,), (0,)), HIGHEST)
    coeffs = dot(inverse, weights, ((0,), (0,)), HIGHEST)
    r_ref[...] = factor_ref[...] * norm_scale
    w_ref[...] = weights * norm_scale
    coeff_high, coeff_low = split(coeffs)
    writes = []
    for i in range(blocks):
        rows = pl.ds(i * block_rows, block_rows)
        high, low = split_ref[rows, :width], split_ref[rows, width:]
        contract = ((1,), (0,))
        product = dot(high, coeff_high, contract)
        product += dot(high, coeff_low, contract) + dot(low, coeff_high, contract)
        reads[i].wait()
        result[i] = buffer[i] - product
        write = pltpu.make_async_copy(result.at[i], remainder_ref.at[rows], out_sems.at[i])
        write.start()
        writes.append(write)
    for write in writes:
        write.wait()


def swap(value, axis, bit):
    size = lax.axis_size(axis)
    return lax.ppermute(value, axis, [(i, i ^ bit) for i in range(size)])


def bits_of(axis):
    size = lax.axis_size(axis)
    assert size & (size - 1) == 0
    return [1 << b for b in range(size.bit_length() - 1)]


def body(panel_block, trailing):
    row_bits, col_bits = bits_of("row"), bits_of("col")
    piece_rows, width = panel_block.shape
    trailing_rows, columns = trailing.shape
    half = width // 2
    total_rows = trailing_rows * lax.axis_size("row")
    norm_scale = 1.0 / math.sqrt(total_rows)
    place = jnp.stack([lax.axis_index("col"), lax.axis_index("row") & 1])

    pieces, order = [panel_block], [0]
    for bit in reversed(col_bits):
        pieces = pieces + [swap(piece, "col", bit) for piece in pieces]
        order = order + [o ^ bit for o in order]

    gram = pl.pallas_call(
        gram_kernel, out_shape=f32(width, width), in_specs=[VMEM], out_specs=VMEM,
        compiler_params=limit(4), name="gram",
    )(panel_block)
    for axis, bit in [("col", col_bits[0])] + [("row", b) for b in row_bits] + [("col", b) for b in col_bits[1:]]:
        gram = gram + swap(gram, axis, bit)
    factor, inverse = pl.pallas_call(
        functools.partial(factor_kernel, block=32, step=8),
        out_shape=(f32(width, width), f32(width, width)),
        in_specs=[VMEM], out_specs=(VMEM, VMEM), compiler_params=limit(4), name="factor",
    )(gram)

    mine, other, panel_split = pl.pallas_call(
        functools.partial(cross_kernel, order=tuple(order)),
        out_shape=(
            f32(half, columns), f32(half, columns),
            jax.ShapeDtypeStruct((trailing_rows, 2 * width), jnp.bfloat16),
        ),
        in_specs=[SMEM] + [VMEM] * len(order) + [ANY],
        out_specs=(VMEM, VMEM, VMEM),
        scratch_shapes=[
            pltpu.VMEM((len(order), piece_rows, columns), jnp.float32),
            pltpu.VMEM((width, columns), jnp.float32),
            pltpu.SemaphoreType.DMA((len(order),)),
        ],
        compiler_params=limit(20),
        name="cross",
    )(place, *pieces, trailing)
    mine = mine + swap(other, "row", row_bits[0])
    for bit in row_bits[1:]:
        mine = mine + swap(mine, "row", bit)
    other = swap(mine, "row", row_bits[0])

    blocks = 8
    return pl.pallas_call(
        functools.partial(final_kernel, norm_scale=norm_scale),
        out_shape=(f32(width, width), f32(width, columns), f32(trailing_rows, columns)),
        in_specs=[SMEM] + [VMEM] * 5 + [ANY],
        out_specs=(VMEM, VMEM, ANY),
        scratch_shapes=[
            pltpu.VMEM((blocks, trailing_rows // blocks, columns), jnp.float32),
            pltpu.VMEM((blocks, trailing_rows // blocks, columns), jnp.float32),
            pltpu.SemaphoreType.DMA((blocks,)),
            pltpu.SemaphoreType.DMA((blocks,)),
        ],
        compiler_params=limit(20),
        name="final",
    )(place, factor, inverse, mine, other, panel_split, trailing)


def solution(mesh):
    in_specs = (P(("row", "col"), None), P("row", "col"))
    out_specs = (P(), P(None, "col"), P("row", "col"))
    return jax.shard_map(body, mesh=mesh, in_specs=in_specs, out_specs=out_specs, check_vma=False)
```

time: 902 us -> 55.6 us (0.06); the launches traced: 886 us -> 55.4 us
  matrix products: 425 us -> 0 us
  other arithmetic: 215 us -> 0.18 us
  waiting for transfers between devices: 126 us -> 20.5 us
  loops' own time: 94.2 us -> 0 us
  starting transfers between devices: 0.12 us -> 18 us
  between operations: 15.5 us -> 0.71 us
  Pallas kernels: 0 us -> 12.8 us
    dot_general x389 -> x0, matrix products: 425 us -> none  [the longest x128 209 us: column_step(): column = jnp.dot(remaining, picker, precision=lax.Precision.HIGHEST)]
    add x256 -> x8, other arithmetic: 213 us -> 0.11 us  [the longest x5 0.05 us: body(): gram = gram + swap(gram, axis, bit)]
    psum x2 -> x0, waiting for transfers between devices: 125 us -> none  [the longest x1 125 us: body(): gram = lax.psum(local_gram, ('row', 'col'))]
    another operation x2 -> x0, loops' own time: 94.2 us -> none  [the longest x1 89.8 us: upper_factor(): remaining, lower = lax.fori_loop(0, width, column_step, start)]
    ppermute x0 -> x12, waiting for transfers between devices: none -> 20.5 us  [swap(): return lax.ppermute(value, axis, [(i, i ^ bit) for i in range(size)])]
    ppermute x0 -> x12, starting transfers between devices: none -> 18 us  [swap(): return lax.ppermute(value, axis, [(i, i ^ bit) for i in range(size)])]
    pallas_call x0 -> x4, Pallas kernels: none -> 12.8 us  [the longest x1 6.06 us: body(): pl.pallas_call(functools.partial(final_kernel, norm_scale=norm_scale), ou...]
  transfers between devices with their start and end apart: 3 -> 12, of which waited for: 1 -> 7; matrix products, arithmetic and copies ran while one was open for 71% -> 0% of each run, Pallas kernels for 0% -> 8%
where the time goes in v1:
time: 55.6 us; the launch traced here: 55.4 us
  waiting for transfers between devices  20.5 us (37%)
  starting transfers between devices  18 us (32%)
  Pallas kernels  12.8 us (23%)
  local copies, waits for them, and re-layouts  3.14 us (6%)
  between operations  0.71 us (1%)
    ppermute x12, waiting for transfers between devices, swap(): return lax.ppermute(value, axis, [(i, i ^ bit) for i in range(size)])  20.5 us
    ppermute x12, starting transfers between devices, swap(): return lax.ppermute(value, axis, [(i, i ^ bit) for i in range(size)])  18 us
    pallas_call x1, Pallas kernels, body(): pl.pallas_call(functools.partial(final_kernel, norm_scale=norm_scale), ou...  6.06 us
    pallas_call x1, Pallas kernels, body(): pl.pallas_call(functools.partial(factor_kernel, block=32, step=8), out_sh...  3.93 us
    unnamed x6, local copies, waits for them, and re-layouts  3.14 us
    pallas_call x1, Pallas kernels, body(): pl.pallas_call(functools.partial(cross_kernel, order=tuple(order)), out_s...  2.44 us
  transfers between devices with their start and end apart: 12, of which 7 were waited for; matrix products, arithmetic and copies ran while one was open for 0% of the time, Pallas kernels for 8%

profile of v1, /device:TPU:0, one launch (start us, length us, event | category | flops | bytes accessed | tf_op | source)
XLA Modules:
  0.0 55.4 jit_solution(7014267680915282598)
XLA Ops:
  0.6 3.0 %collective-permute-start.5 = (f32[512,128]{1,0:T(8,128)}, f32[512,128]{1,0:T(8,128)S(1)}, u32[]{:S(2)}, u32[]{:S(2)}) collective-permute-start(f32[512,128]{1,0:T(8,128)} %refs_0_.1), channel_id=1, source_target_pairs={{0,2},{1,3},{2,0},{3,1},{4,6},{5,7},{6,4},{7,5},{8,10},{9,11},{10,... | collective-permute-start | bytes 786440 | tf_op jit(solution)/shard_map/ppermute | solution.py:157
  3.7 0.0 collective-permute-start.6
  3.7 6.5 %collective-permute-done.5.refs_1_ = f32[512,128]{1,0:T(8,128)S(1)} collective-permute-done((f32[512,128]{1,0:T(8,128)}, f32[512,128]{1,0:T(8,128)S(1)}, u32[]{:S(2)}, u32[]{:S(2)}) %collective-permute-start.5) | collective-permute-done | bytes 262176 | tf_op jit(solution)/shard_map/ppermute | solution.py:157
  10.2 0.0 collective-permute-start.7
  10.2 0.1 pad_add_fusion.place_ref
  10.3 0.0 collective-permute-done.6.refs_2_
  10.3 1.5 %collective-permute-done.7.refs_3_ = f32[512,128]{1,0:T(8,128)S(1)} collective-permute-done((f32[512,128]{1,0:T(8,128)S(1)}, f32[512,128]{1,0:T(8,128)S(1)}, u32[]{:S(2)}, u32[]{:S(2)}) %collective-permute-start.7) | collective-permute-done | bytes 262176 | tf_op jit(solution)/shard_map/ppermute | solution.py:157
  11.7 2.2 %copy-done = f32[2048,512]{1,0:T(8,128)S(1)} copy-done((f32[2048,512]{1,0:T(8,128)S(1)}, f32[2048,512]{1,0:T(8,128)}, u32[]{:S(2)}) %copy-start) | copy-done | bytes 4194328
  13.9 0.9 %copy-done.2 = f32[512,128]{1,0:T(8,128)S(1)} copy-done((f32[512,128]{1,0:T(8,128)S(1)}, f32[512,128]{1,0:T(8,128)}, u32[]{:S(2)}) %copy-start.2) | copy-done | bytes 262168
  14.9 2.4 %cross.1 = (f32[64,512]{1,0:T(8,128)S(1)}, f32[64,512]{1,0:T(8,128)S(1)}, bf16[2048,256]{1,0:T(8,128)(2,1)S(1)}) custom-call(s32[2]{0:T(128)S(1)} %pad_add_fusion.place_ref, f32[512,128]{1,0:T(8,128)S(1)} %copy-done.2, f32[512,128]{1,0:T(8,128)S(1)} %collective-permute-done.5.refs_1_, f32[512,128]{1,0:T(8,128)S(1)} %collective-permute-done.6.refs_2_, ...), custom_call_target="tpu_custom_call" | custom-call | tf_op jit(solution)/shard_map/cross/pallas_call | solution.py:192
  17.3 1.8 %collective-permute-start.8 = (f32[64,512]{1,0:T(8,128)S(1)}, f32[64,512]{1,0:T(8,128)S(1)}, u32[]{:S(2)}, u32[]{:S(2)}) collective-permute-start(f32[64,512]{1,0:T(8,128)S(1)} %get-tuple-element.11), channel_id=1, source_target_pairs={{0,4},{4,0},{8,12},{12,8},{16,20},{20,16},{24,28},{28,24},{1,5},{5... | collective-permute-start | bytes 393224 | tf_op jit(solution)/shard_map/ppermute | solution.py:157
  19.1 3.8 %collective-permute-done.8 = f32[64,512]{1,0:T(8,128)S(1)} collective-permute-done((f32[64,512]{1,0:T(8,128)S(1)}, f32[64,512]{1,0:T(8,128)S(1)}, u32[]{:S(2)}, u32[]{:S(2)}) %collective-permute-start.8) | collective-permute-done | bytes 131104 | tf_op jit(solution)/shard_map/ppermute | solution.py:157
  23.0 1.9 %collective-permute-start.9 = (f32[64,512]{1,0:T(8,128)S(1)}, f32[64,512]{1,0:T(8,128)S(1)}, u32[]{:S(2)}, u32[]{:S(2)}) collective-permute-start(f32[64,512]{1,0:T(8,128)S(1)} %add.29), channel_id=1, source_target_pairs={{0,8},{4,12},{8,0},{12,4},{16,24},{20,28},{24,16},{28,20},{1,9},{5... | collective-permute-start | bytes 393224 | tf_op jit(solution)/shard_map/ppermute | solution.py:157
  24.8 0.4 gram.1
  25.2 0.1 collective-permute-start
  25.3 1.2 %collective-permute-done = f32[128,128]{1,0:T(8,128)S(1)} collective-permute-done((f32[128,128]{1,0:T(8,128)S(1)}, f32[128,128]{1,0:T(8,128)S(1)}, u32[]{:S(2)}, u32[]{:S(2)}) %collective-permute-start) | collective-permute-done | bytes 65568 | tf_op jit(solution)/shard_map/ppermute | solution.py:157
  26.6 1.6 %collective-permute-start.1 = (f32[128,128]{1,0:T(8,128)S(1)}, f32[128,128]{1,0:T(8,128)S(1)}, u32[]{:S(2)}, u32[]{:S(2)}) collective-permute-start(f32[128,128]{1,0:T(8,128)S(1)} %add.24), channel_id=1, source_target_pairs={{0,4},{4,0},{8,12},{12,8},{16,20},{20,16},{24,28},{28,24},{1,5},{5... | collective-permute-start | bytes 196616 | tf_op jit(solution)/shard_map/ppermute | solution.py:157
  28.2 0.0 collective-permute-done.9
  28.2 2.7 %collective-permute-start.10 = (f32[64,512]{1,0:T(8,128)S(1)}, f32[64,512]{1,0:T(8,128)S(1)}, u32[]{:S(2)}, u32[]{:S(2)}) collective-permute-start(f32[64,512]{1,0:T(8,128)S(1)} %add.30), channel_id=1, source_target_pairs={{0,16},{4,20},{8,24},{12,28},{16,0},{20,4},{24,8},{28,12},{1,17},{... | collective-permute-start | bytes 393224 | tf_op jit(solution)/shard_map/ppermute | solution.py:157
  30.9 0.0 collective-permute-done.1
  30.9 1.6 %collective-permute-start.2 = (f32[128,128]{1,0:T(8,128)S(1)}, f32[128,128]{1,0:T(8,128)S(1)}, u32[]{:S(2)}, u32[]{:S(2)}) collective-permute-start(f32[128,128]{1,0:T(8,128)S(1)} %add.25), channel_id=1, source_target_pairs={{0,8},{4,12},{8,0},{12,4},{16,24},{20,28},{24,16},{28,20},{1,9},{5... | collective-permute-start | bytes 196616 | tf_op jit(solution)/shard_map/ppermute | solution.py:157
  32.5 3.2 %collective-permute-done.2 = f32[128,128]{1,0:T(8,128)S(1)} collective-permute-done((f32[128,128]{1,0:T(8,128)S(1)}, f32[128,128]{1,0:T(8,128)S(1)}, u32[]{:S(2)}, u32[]{:S(2)}) %collective-permute-start.2) | collective-permute-done | bytes 65568 | tf_op jit(solution)/shard_map/ppermute | solution.py:157
  35.8 2.1 %collective-permute-start.3 = (f32[128,128]{1,0:T(8,128)S(1)}, f32[128,128]{1,0:T(8,128)S(1)}, u32[]{:S(2)}, u32[]{:S(2)}) collective-permute-start(f32[128,128]{1,0:T(8,128)S(1)} %add.26), channel_id=1, source_target_pairs={{0,16},{4,20},{8,24},{12,28},{16,0},{20,4},{24,8},{28,12},{1,17},{... | collective-permute-start | bytes 196616 | tf_op jit(solution)/shard_map/ppermute | solution.py:157
  37.9 0.0 collective-permute-done.10
  37.9 1.6 %collective-permute-start.11 = (f32[64,512]{1,0:T(8,128)S(1)}, f32[64,512]{1,0:T(8,128)S(1)}, u32[]{:S(2)}, u32[]{:S(2)}) collective-permute-start(f32[64,512]{1,0:T(8,128)S(1)} %add.31.mine_ref), channel_id=1, source_target_pairs={{0,4},{4,0},{8,12},{12,8},{16,20},{20,16},{24,28},{28,24},{1,5},{5... | collective-permute-start | bytes 393224 | tf_op jit(solution)/shard_map/ppermute | solution.py:157
  39.5 1.5 %collective-permute-done.3 = f32[128,128]{1,0:T(8,128)S(1)} collective-permute-done((f32[128,128]{1,0:T(8,128)S(1)}, f32[128,128]{1,0:T(8,128)S(1)}, u32[]{:S(2)}, u32[]{:S(2)}) %collective-permute-start.3) | collective-permute-done | bytes 65568 | tf_op jit(solution)/shard_map/ppermute | solution.py:157
  41.0 1.5 %collective-permute-start.4 = (f32[128,128]{1,0:T(8,128)S(1)}, f32[128,128]{1,0:T(8,128)S(1)}, u32[]{:S(2)}, u32[]{:S(2)}) collective-permute-start(f32[128,128]{1,0:T(8,128)S(1)} %add.27), channel_id=1, source_target_pairs={{0,2},{1,3},{2,0},{3,1},{4,6},{5,7},{6,4},{7,5},{8,10},{9,11},{10,... | collective-permute-start | bytes 196616 | tf_op jit(solution)/shard_map/ppermute | solution.py:157
  42.6 2.8 %collective-permute-done.4 = f32[128,128]{1,0:T(8,128)S(1)} collective-permute-done((f32[128,128]{1,0:T(8,128)S(1)}, f32[128,128]{1,0:T(8,128)S(1)}, u32[]{:S(2)}, u32[]{:S(2)}) %collective-permute-start.4) | collective-permute-done | bytes 65568 | tf_op jit(solution)/shard_map/ppermute | solution.py:157
  45.4 3.9 %factor.1 = (f32[128,128]{1,0:T(8,128)S(1)}, f32[128,128]{1,0:T(8,128)S(1)}) custom-call(f32[128,128]{1,0:T(8,128)S(1)} %add.28.gram_ref), custom_call_target="tpu_custom_call" | custom-call | tf_op jit(solution)/shard_map/factor/pallas_call | solution.py:186
  49.3 0.0 collective-permute-done.11.other_ref
  49.3 0.0 copy-done.1
  49.3 6.1 %final.1 = (f32[128,128]{1,0:T(8,128)}, f32[128,512]{1,0:T(8,128)}, f32[2048,512]{1,0:T(8,128)}) custom-call(s32[2]{0:T(128)S(1)} %pad_add_fusion.place_ref, f32[128,128]{1,0:T(8,128)S(1)} %get-tuple-element.8.factor_ref, f32[128,128]{1,0:T(8,128)S(1)} %get-tuple-element.9.inverse_ref, f32[64,512]{1,0:T(8,128)S(1)} %add.31.mine_ref, ...), custom_call_target="tpu_custom_call" | custom-call | tf_op jit(solution)/shard_map/final/pallas_call | solution.py:214
  (11 shorter events, 0.1 us)
Async XLA Ops:
  0.6 9.6 %collective-permute-start.5 = (f32[512,128]{1,0:T(8,128)}, f32[512,128]{1,0:T(8,128)S(1)}, u32[]{:S(2)}, u32[]{:S(2)}) collective-permute-start(f32[512,128]{1,0:T(8,128)} %refs_0_.1), channel_id=1, source_target_pairs={{0,2},{1,3},{2,0},{3,1},{4,6},{5,7},{6,4},{7,5},{8,10},{9,11},{10,... | collective-permute-start | bytes 786440 | tf_op jit(solution)/shard_map/ppermute | solution.py:157
  3.7 6.6 %collective-permute-start.6 = (f32[512,128]{1,0:T(8,128)}, f32[512,128]{1,0:T(8,128)S(1)}, u32[]{:S(2)}, u32[]{:S(2)}) collective-permute-start(f32[512,128]{1,0:T(8,128)} %refs_0_.1), channel_id=1, source_target_pairs={{0,1},{1,0},{2,3},{3,2},{4,5},{5,4},{6,7},{7,6},{8,9},{9,8},{10,11... | collective-permute-start | bytes 786440 | tf_op jit(solution)/shard_map/ppermute | solution.py:157
  10.2 1.5 %collective-permute-start.7 = (f32[512,128]{1,0:T(8,128)S(1)}, f32[512,128]{1,0:T(8,128)S(1)}, u32[]{:S(2)}, u32[]{:S(2)}) collective-permute-start(f32[512,128]{1,0:T(8,128)S(1)} %collective-permute-done.5.refs_1_), channel_id=1, source_target_pairs={{0,1},{1,0},{2,3},{3,2},{4,5},{5,4},{6,7},{7,6},{8,9},{9,8},{10,11... | collective-permute-start | bytes 786440 | tf_op jit(solution)/shard_map/ppermute | solution.py:157
  11.7 2.2 %copy-start = (f32[2048,512]{1,0:T(8,128)S(1)}, f32[2048,512]{1,0:T(8,128)}, u32[]{:S(2)}) copy-start(f32[2048,512]{1,0:T(8,128)} %trailing_ref.1) | copy-start | bytes 12582916
  13.9 0.9 %copy-start.2 = (f32[512,128]{1,0:T(8,128)S(1)}, f32[512,128]{1,0:T(8,128)}, u32[]{:S(2)}) copy-start(f32[512,128]{1,0:T(8,128)} %refs_0_.1) | copy-start | bytes 786436
  14.9 34.4 %copy-start.1 = (f32[2048,512]{1,0:T(8,128)S(1)}, f32[2048,512]{1,0:T(8,128)}, u32[]{:S(2)}) copy-start(f32[2048,512]{1,0:T(8,128)} %trailing_ref.1) | copy-start | bytes 12582916
  17.3 5.6 %collective-permute-start.8 = (f32[64,512]{1,0:T(8,128)S(1)}, f32[64,512]{1,0:T(8,128)S(1)}, u32[]{:S(2)}, u32[]{:S(2)}) collective-permute-start(f32[64,512]{1,0:T(8,128)S(1)} %get-tuple-element.11), channel_id=1, source_target_pairs={{0,4},{4,0},{8,12},{12,8},{16,20},{20,16},{24,28},{28,24},{1,5},{5... | collective-permute-start | bytes 393224 | tf_op jit(solution)/shard_map/ppermute | solution.py:157
  23.0 5.2 %collective-permute-start.9 = (f32[64,512]{1,0:T(8,128)S(1)}, f32[64,512]{1,0:T(8,128)S(1)}, u32[]{:S(2)}, u32[]{:S(2)}) collective-permute-start(f32[64,512]{1,0:T(8,128)S(1)} %add.29), channel_id=1, source_target_pairs={{0,8},{4,12},{8,0},{12,4},{16,24},{20,28},{24,16},{28,20},{1,9},{5... | collective-permute-start | bytes 393224 | tf_op jit(solution)/shard_map/ppermute | solution.py:157
  25.2 1.3 %collective-permute-start = (f32[128,128]{1,0:T(8,128)S(1)}, f32[128,128]{1,0:T(8,128)S(1)}, u32[]{:S(2)}, u32[]{:S(2)}) collective-permute-start(f32[128,128]{1,0:T(8,128)S(1)} %gram.1), channel_id=1, source_target_pairs={{0,1},{1,0},{2,3},{3,2},{4,5},{5,4},{6,7},{7,6},{8,9},{9,8},{10,11... | collective-permute-start | bytes 196616 | tf_op jit(solution)/shard_map/ppermute | solution.py:157
  26.6 4.3 %collective-permute-start.1 = (f32[128,128]{1,0:T(8,128)S(1)}, f32[128,128]{1,0:T(8,128)S(1)}, u32[]{:S(2)}, u32[]{:S(2)}) collective-permute-start(f32[128,128]{1,0:T(8,128)S(1)} %add.24), channel_id=1, source_target_pairs={{0,4},{4,0},{8,12},{12,8},{16,20},{20,16},{24,28},{28,24},{1,5},{5... | collective-permute-start | bytes 196616 | tf_op jit(solution)/shard_map/ppermute | solution.py:157
  28.2 9.7 %collective-permute-start.10 = (f32[64,512]{1,0:T(8,128)S(1)}, f32[64,512]{1,0:T(8,128)S(1)}, u32[]{:S(2)}, u32[]{:S(2)}) collective-permute-start(f32[64,512]{1,0:T(8,128)S(1)} %add.30), channel_id=1, source_target_pairs={{0,16},{4,20},{8,24},{12,28},{16,0},{20,4},{24,8},{28,12},{1,17},{... | collective-permute-start | bytes 393224 | tf_op jit(solution)/shard_map/ppermute | solution.py:157
  30.9 4.8 %collective-permute-start.2 = (f32[128,128]{1,0:T(8,128)S(1)}, f32[128,128]{1,0:T(8,128)S(1)}, u32[]{:S(2)}, u32[]{:S(2)}) collective-permute-start(f32[128,128]{1,0:T(8,128)S(1)} %add.25), channel_id=1, source_target_pairs={{0,8},{4,12},{8,0},{12,4},{16,24},{20,28},{24,16},{28,20},{1,9},{5... | collective-permute-start | bytes 196616 | tf_op jit(solution)/shard_map/ppermute | solution.py:157
  35.8 5.2 %collective-permute-start.3 = (f32[128,128]{1,0:T(8,128)S(1)}, f32[128,128]{1,0:T(8,128)S(1)}, u32[]{:S(2)}, u32[]{:S(2)}) collective-permute-start(f32[128,128]{1,0:T(8,128)S(1)} %add.26), channel_id=1, source_target_pairs={{0,16},{4,20},{8,24},{12,28},{16,0},{20,4},{24,8},{28,12},{1,17},{... | collective-permute-start | bytes 196616 | tf_op jit(solution)/shard_map/ppermute | solution.py:157
  37.9 11.3 %collective-permute-start.11 = (f32[64,512]{1,0:T(8,128)S(1)}, f32[64,512]{1,0:T(8,128)S(1)}, u32[]{:S(2)}, u32[]{:S(2)}) collective-permute-start(f32[64,512]{1,0:T(8,128)S(1)} %add.31.mine_ref), channel_id=1, source_target_pairs={{0,4},{4,0},{8,12},{12,8},{16,20},{20,16},{24,28},{28,24},{1,5},{5... | collective-permute-start | bytes 393224 | tf_op jit(solution)/shard_map/ppermute | solution.py:157
  41.0 4.3 %collective-permute-start.4 = (f32[128,128]{1,0:T(8,128)S(1)}, f32[128,128]{1,0:T(8,128)S(1)}, u32[]{:S(2)}, u32[]{:S(2)}) collective-permute-start(f32[128,128]{1,0:T(8,128)S(1)} %add.27), channel_id=1, source_target_pairs={{0,2},{1,3},{2,0},{3,1},{4,6},{5,7},{6,4},{7,5},{8,10},{9,11},{10,... | collective-permute-start | bytes 196616 | tf_op jit(solution)/shard_map/ppermute | solution.py:157

commit v2 on v0

v2 whole, which is shorter than its diff:
```python
import functools
import math

import jax
import jax.numpy as jnp
from jax import lax
from jax.experimental import pallas as pl
from jax.experimental.pallas import tpu as pltpu
from jax.sharding import PartitionSpec as P


HIGHEST = lax.Precision.HIGHEST
ROOM = 48
CUTS = 4
VMEM = pl.BlockSpec(memory_space=pltpu.VMEM)
HBM = pl.BlockSpec(memory_space=pltpu.HBM)


def limit(mebibytes):
    return pltpu.CompilerParams(vmem_limit_bytes=mebibytes << 20)


def f32(*shape):
    return jax.ShapeDtypeStruct(shape, jnp.float32)


def split(value):
    high = value.astype(jnp.bfloat16)
    return high, (value - high.astype(jnp.float32)).astype(jnp.bfloat16)


def store_split(split_ref, piece):
    width = piece.shape[1]
    split_ref[:, :width], split_ref[:, width:] = split(piece)


def cross_of(split_ref, block):
    width = split_ref.shape[1] // 2
    high, low = split_ref[:, :width], split_ref[:, width:]
    block_high, block_low = split(block)
    contract = ((0,), (0,))
    product = dot(high, block_high, contract)
    return product + dot(high, block_low, contract) + dot(low, block_high, contract)


def dot(first, second, dims, precision=None):
    return lax.dot_general(
        first, second, (dims, ((), ())), precision=precision, preferred_element_type=jnp.float32
    )


def block_of(offset, rows):
    return (lax.axis_index("col") ^ offset) * rows


def copy_in(source, first, target, sems):
    rows = target.shape[0] // CUTS
    copies = []
    for k in range(CUTS):
        where = pl.ds(pl.multiple_of(first + k * rows, rows), rows)
        copies.append(pltpu.make_async_copy(source.at[where], target.at[pl.ds(k * rows, rows)], sems.at[k]))
        copies[-1].start()
    return copies


def part_of(offset, group):
    return (lax.axis_index("row") & (group - 1)) ^ offset


def wait_all(copies):
    for copy in copies:
        copy.wait()


def own_kernel(panel_ref, gram_ref, split_ref):
    panel = panel_ref[...]
    gram_ref[...] = dot(panel, panel, ((0,), (0,)), HIGHEST)
    store_split(split_ref, panel)


def mate_kernel(mate_ref, gram_in_ref, gram_ref, split_ref, sum_ref, *, near):
    mate = mate_ref[...]
    half = mate.shape[1] // 2
    sum_ref[...] = gram_in_ref[...] + dot(mate, mate, ((0,), (0,)), HIGHEST)
    upper = jnp.where((lax.axis_index("col") & near) == 0, 0, half)
    gram_ref[...] = sum_ref[pl.ds(pl.multiple_of(upper, half), half), :]
    store_split(split_ref, mate)


def near_kernel(own_ref, mate_ref, trailing_ref, cross_ref, *refs, order):
    held_refs, sems = refs[: len(order)], refs[len(order)]
    rows = own_ref.shape[0]
    copies = [
        copy_in(trailing_ref, block_of(offset, rows), held_ref, sems.at[i])
        for i, (offset, held_ref) in enumerate(zip(order, held_refs))
    ]
    wait_all(copies[0])
    total = cross_of(own_ref, held_refs[0][...])
    wait_all(copies[1])
    cross_ref[...] = total + cross_of(mate_ref, held_refs[1][...])
    for rest in copies[2:]:
        wait_all(rest)


def far_kernel(piece_ref, held_ref, cross_in_ref, split_ref, cross_ref):
    store_split(split_ref, piece_ref[...])
    cross_ref[...] = cross_in_ref[...] + cross_of(split_ref, held_ref[...])


def last_kernel(piece_ref, held_ref, cross_in_ref, split_ref, *refs):
    *part_refs, sum_ref = refs
    store_split(split_ref, piece_ref[...])
    sum_ref[...] = cross_in_ref[...] + cross_of(split_ref, held_ref[...])
    part = part_refs[0].shape[1]
    for k, part_ref in enumerate(part_refs):
        first = pl.multiple_of(part_of(k, len(part_refs)) * part, part)
        part_ref[...] = sum_ref[:, pl.ds(first, part)]


def factor_kernel(mine_ref, other_ref, scaled_ref, solve_ref, *, near, block, step, norm_scale):
    width = mine_ref.shape[1]
    first_half = (lax.axis_index("col") & near) == 0
    mine, other = mine_ref[...], other_ref[...]
    gram = jnp.concatenate(
        [jnp.where(first_half, mine, other), jnp.where(first_half, other, mine)], 0
    )
    local = lax.broadcasted_iota(jnp.int32, (step, 1), 0)
    lanes = lax.broadcasted_iota(jnp.int32, (block, width), 1)
    rows = lax.broadcasted_iota(jnp.int32, (block, width), 0)
    factor_rows, inverse_rows = [], []
    for first in range(0, width, block):
        left = gram[first : first + block, :]
        right = jnp.where(lanes == rows + first, 1.0, 0.0)
        if factor_rows:
            above = jnp.concatenate(factor_rows, 0)
            both = jnp.concatenate([above, jnp.concatenate(inverse_rows, 0)], 1)
            update = dot(above[:, first : first + block], both, ((0,), (0,)), HIGHEST)
            left = left - update[:, :width]
            right = right - update[:, width:]
        left_done, right_done = [], []
        for start in range(first, first + block, step):
            columns = [
                jnp.broadcast_to(left[:, start + j : start + j + 1], left.shape) for j in range(step)
            ]
            pivots = jnp.ones((step, width), jnp.float32)
            for k in range(step):
                pivot = columns[k][k : k + 1, :]
                pivots = jnp.where(local == k, pivot, pivots)
                ratio = columns[k] * (1.0 / pivot)
                head = jnp.where(local > k, ratio[:step], 0.0)
                if ratio.shape[0] > step:
                    head = jnp.concatenate([head, ratio[step:]], 0)
                ratio = head
                for j in range(k + 1, step):
                    columns[j] = columns[j] - ratio * columns[j][k : k + 1, :]
                left = left - ratio * left[k : k + 1, :]
                right = right - ratio * right[k : k + 1, :]
            scale = lax.rsqrt(pivots)
            left_done.append(left[:step] * scale)
            right_done.append(right[:step] * scale)
            left, right = left[step:], right[step:]
        factor_rows.append(jnp.where(lanes >= rows + first, jnp.concatenate(left_done, 0), 0.0))
        inverse_rows.append(jnp.where(lanes <= rows + first, jnp.concatenate(right_done, 0), 0.0))
        scaled_ref[first : first + block, :] = factor_rows[-1] * norm_scale
    inverse = jnp.concatenate(inverse_rows, 0)
    solve = jnp.concatenate([inverse, dot(inverse, inverse, ((0,), (0,)), HIGHEST)], 0)
    store_split(solve_ref, solve)


def basis_kernel(solve_ref, *refs):
    *split_refs, out_ref = refs
    width = solve_ref.shape[1] // 2
    high, low = solve_ref[width:, :width], solve_ref[width:, width:]
    right = jnp.concatenate([high, high, low], 0)
    rows = split_refs[0].shape[0]
    for i, split_ref in enumerate(split_refs):
        both = split_ref[...]
        left = jnp.concatenate([both, both[:, :width]], 1)
        store_split(out_ref.at[i * rows : (i + 1) * rows], dot(left, right, ((1,), (0,))))


def final_kernel(solve_ref, basis_ref, *refs, order, parts, group, norm_scale, chunk, last):
    held_refs, refs = refs[: len(order)], refs[len(order) :]
    cross_refs, refs = refs[: len(parts)], refs[len(parts) :]
    if last:
        w_before_ref, _, w_ref, remainder_ref, result, sems = refs
    else:
        w_ref, remainder_ref, result, sems = refs
    width, part = cross_refs[0].shape
    cross = jnp.concatenate([ref[...] for ref in cross_refs], 1)
    high, low = split(cross)
    right = jnp.concatenate([high, high, low], 0)
    contract = ((1,), (0,))
    columns = [pl.ds(pl.multiple_of(part_of(k, group) * part, part), part) for k in parts]
    writes = []
    for i, held_ref in enumerate(held_refs):
        rows = held_ref.shape[0]
        where = pl.ds(pl.multiple_of(block_of(order[i], rows), rows), rows)
        for first in range(0, rows, chunk):
            here = slice(first, first + chunk)
            both = basis_ref[i * rows + first : i * rows + first + chunk, :]
            product = dot(jnp.concatenate([both, both[:, :width]], 1), right, contract)
            for j, column in enumerate(columns):
                result[i, j, here, :] = held_ref[here, column] - product[:, j * part : (j + 1) * part]
        for j, column in enumerate(columns):
            write = pltpu.make_async_copy(
                result.at[i, j], remainder_ref.at[where, column], sems.at[i, j]
            )
            write.start()
            writes.append(write)
    inverse = solve_ref[:width, :]
    weights = dot(jnp.concatenate([inverse, inverse[:, :width]], 1), right, contract) * norm_scale
    if last:
        w_ref[...] = w_before_ref[...]
    for j, column in enumerate(columns):
        w_ref[:, column] = weights[:, j * part : (j + 1) * part]
    wait_all(writes)


def swap(value, axis, bit):
    size = lax.axis_size(axis)
    return lax.ppermute(value, axis, [(i, i ^ bit) for i in range(size)])


def bits_of(axis):
    size = lax.axis_size(axis)
    assert size & (size - 1) == 0
    return [1 << b for b in range(size.bit_length() - 1)]


def body(panel_block, trailing):
    row_bits, col_bits = bits_of("row"), bits_of("col")
    near, far_bits = col_bits[0], col_bits[1:]
    piece_rows, width = panel_block.shape
    trailing_rows, columns = trailing.shape
    group_bits = row_bits[:2]
    group = 1 << len(group_bits)
    part = columns // group
    total_rows = trailing_rows * lax.axis_size("row")
    norm_scale = 1.0 / math.sqrt(total_rows)

    far, offsets = [panel_block], [0]
    for bit in far_bits:
        far = far + [swap(piece, "col", bit) for piece in far]
        offsets = offsets + [o ^ bit for o in offsets]
    mate = swap(panel_block, "col", near)
    last = [swap(piece, "col", near) for piece in far[1:]]
    order = [0, near] + offsets[1:] + [o ^ near for o in offsets[1:]]

    square, wide = f32(width, width), f32(width, columns)
    half_square, block = f32(width // 2, width), f32(piece_rows, columns)
    split_shape = jax.ShapeDtypeStruct((piece_rows, 2 * width), jnp.bfloat16)
    copies = pltpu.SemaphoreType.DMA
    gram, own_split = pl.pallas_call(
        own_kernel, out_shape=(square, split_shape), in_specs=[VMEM], out_specs=(VMEM,) * 2,
        compiler_params=limit(8), name="own",
    )(panel_block)
    gram, mate_split = pl.pallas_call(
        functools.partial(mate_kernel, near=near),
        out_shape=(half_square, split_shape), in_specs=[VMEM] * 2, out_specs=(VMEM,) * 2,
        scratch_shapes=[pltpu.VMEM((width, width), jnp.float32)],
        compiler_params=limit(8), name="mate",
    )(mate, gram)
    cross, *held = pl.pallas_call(
        functools.partial(near_kernel, order=order),
        out_shape=(wide,) + (block,) * len(order),
        in_specs=[VMEM, VMEM, HBM], out_specs=(VMEM,) * (1 + len(order)),
        scratch_shapes=[copies((len(order), CUTS))], compiler_params=limit(ROOM), name="near",
    )(own_split, mate_split, trailing)
    splits = [own_split, mate_split]
    pieces = far[1:] + last
    for i, piece in enumerate(pieces[:-1]):
        split_out, cross = pl.pallas_call(
            far_kernel, out_shape=(split_shape, wide), in_specs=[VMEM] * 3,
            out_specs=(VMEM,) * 2, compiler_params=limit(16), name="far",
        )(piece, held[i + 2], cross)
        splits.append(split_out)
    split_out, *parts = pl.pallas_call(
        last_kernel,
        out_shape=(split_shape,) + (f32(width, part),) * group,
        in_specs=[VMEM] * 3, out_specs=(VMEM,) * (1 + group),
        scratch_shapes=[pltpu.VMEM((width, columns), jnp.float32)],
        compiler_params=limit(16), name="last",
    )(pieces[-1], held[-1], cross)
    splits.append(split_out)

    gram = gram + sum(swap(gram, "row", k) for k in range(1, group))
    for axis, bit in [("row", b) for b in row_bits[len(group_bits) :]] + [("col", b) for b in far_bits]:
        gram = gram + swap(gram, axis, bit)
    other_half = swap(gram, "col", near)
    r_scaled, solve = pl.pallas_call(
        functools.partial(factor_kernel, near=near, block=32, step=8, norm_scale=norm_scale),
        out_shape=(square, jax.ShapeDtypeStruct((2 * width, 2 * width), jnp.bfloat16)),
        in_specs=[VMEM, VMEM], out_specs=(VMEM, VMEM), compiler_params=limit(4), name="factor",
    )(gram, other_half)
    mine = parts[0]
    for k in range(1, group):
        mine = mine + swap(parts[k], "row", k)
    for bit in row_bits[len(group_bits) :]:
        mine = mine + swap(mine, "row", bit)
    others = [swap(mine, "row", k) for k in range(1, group)]

    basis = pl.pallas_call(
        basis_kernel,
        out_shape=jax.ShapeDtypeStruct((trailing_rows, 2 * width), jnp.bfloat16),
        in_specs=[VMEM] * (1 + len(splits)), out_specs=VMEM, compiler_params=limit(8), name="basis",
    )(solve, *splits)
    def final(ks, *before):
        given = [mine, *others]
        operands = (solve, basis, *held, *[given[k] for k in ks])
        return pl.pallas_call(
            functools.partial(
                final_kernel, order=order, parts=ks, group=group, norm_scale=norm_scale,
                chunk=128, last=bool(before),
            ),
            out_shape=(wide, f32(trailing_rows, columns)),
            in_specs=[VMEM] * len(operands) + [VMEM, HBM][: len(before)], out_specs=(VMEM, HBM),
            scratch_shapes=[
                pltpu.VMEM((len(order), len(ks), piece_rows, part), jnp.float32),
                copies((len(order), len(ks))),
            ],
            input_output_aliases={len(operands) + 1: 1} if before else {},
            compiler_params=limit(20),
        )(*operands, *before)

    first = (0, group - 1)
    before = final(first)
    rest = tuple(k for k in range(group) if k not in first)
    w_scaled, remainder = final(rest, *before) if rest else before
    return r_scaled, w_scaled, remainder


def solution(mesh):
    in_specs = (P(("row", "col"), None), P("row", "col"))
    out_specs = (P(), P(None, "col"), P("row", "col"))

    return jax.shard_map(body, mesh=mesh, in_specs=in_specs, out_specs=out_specs, check_vma=False)
```

time: 902 us -> 48 us (0.05); the launches traced: 886 us -> 47.9 us
  matrix products: 425 us -> 0 us
  other arithmetic: 215 us -> 0.05 us
  waiting for transfers between devices: 126 us -> 13.2 us
  loops' own time: 94.2 us -> 0 us
  starting transfers between devices: 0.12 us -> 19.5 us
  between operations: 15.5 us -> 0.76 us
  Pallas kernels: 0 us -> 13.4 us
  local copies, waits for them, and re-layouts: 10.8 us -> 0.95 us
    dot_general x389 -> x0, matrix products: 425 us -> none  [the longest x128 209 us: column_step(): column = jnp.dot(remaining, picker, precision=lax.Precision.HIGHEST)]
    add x256 -> x5, other arithmetic: 213 us -> 0.05 us  [the longest x1 0.02 us: body(): mine = mine + swap(parts[k], 'row', k)]
    psum x2 -> x0, waiting for transfers between devices: 125 us -> none  [the longest x1 125 us: body(): gram = lax.psum(local_gram, ('row', 'col'))]
    another operation x2 -> x0, loops' own time: 94.2 us -> none  [the longest x1 89.8 us: upper_factor(): remaining, lower = lax.fori_loop(0, width, column_step, start)]
    ppermute x0 -> x16, starting transfers between devices: none -> 19.5 us  [swap(): return lax.ppermute(value, axis, [(i, i ^ bit) for i in range(size)])]
    pallas_call x0 -> x9, Pallas kernels: none -> 13.4 us  [the longest x1 4.6 us: body(): pl.pallas_call(functools.partial(factor_kernel, near=near, block=32, step...]
    ppermute x0 -> x16, waiting for transfers between devices: none -> 13.2 us  [swap(): return lax.ppermute(value, axis, [(i, i ^ bit) for i in range(size)])]
    unnamed x4 -> x2, local copies, waits for them, and re-layouts: 10.7 us -> 0.95 us
  transfers between devices with their start and end apart: 3 -> 16, of which waited for: 1 -> 4; matrix products, arithmetic and copies ran while one was open for 71% -> 0% of each run, Pallas kernels for 0% -> 22%
where the time goes in v2:
time: 48 us; the launch traced here: 47.9 us
  starting transfers between devices  19.5 us (41%)
  Pallas kernels  13.4 us (28%)
  waiting for transfers between devices  13.2 us (28%)
  local copies, waits for them, and re-layouts  0.95 us (2%)
  between operations  0.76 us (2%)
    ppermute x16, starting transfers between devices, swap(): return lax.ppermute(value, axis, [(i, i ^ bit) for i in range(size)])  19.5 us
    ppermute x16, waiting for transfers between devices, swap(): return lax.ppermute(value, axis, [(i, i ^ bit) for i in range(size)])  13.2 us
    pallas_call x1, Pallas kernels, body(): pl.pallas_call(functools.partial(factor_kernel, near=near, block=32, step...  4.6 us
    pallas_call x2, Pallas kernels, final(): pl.pallas_call(functools.partial(final_kernel, order=order, parts=ks, gro...  4.14 us
    pallas_call x1, Pallas kernels, body(): pl.pallas_call(functools.partial(near_kernel, order=order), out_shape=(wi...  2.29 us
  transfers between devices with their start and end apart: 16, of which 4 were waited for; matrix products, arithmetic and copies ran while one was open for 0% of the time, Pallas kernels for 22%

profile of v2, /device:TPU:0, one launch (start us, length us, event | category | flops | bytes accessed | tf_op | source)
XLA Modules:
  0.0 47.9 jit_solution(3392943369437990946)
XLA Ops:
  0.6 3.0 %collective-permute-start.7 = (f32[512,128]{1,0:T(8,128)}, f32[512,128]{1,0:T(8,128)S(1)}, u32[]{:S(2)}, u32[]{:S(2)}) collective-permute-start(f32[512,128]{1,0:T(8,128)} %panel_ref.1), channel_id=1, source_target_pairs={{0,2},{1,3},{2,0},{3,1},{4,6},{5,7},{6,4},{7,5},{8,10},{9,11},{10,... | collective-permute-start | bytes 786440 | tf_op jit(solution)/shard_map/ppermute | solution.py:222
  3.7 0.0 collective-permute-start
  3.7 6.5 %collective-permute-done.7.piece_ref = f32[512,128]{1,0:T(8,128)S(1)} collective-permute-done((f32[512,128]{1,0:T(8,128)}, f32[512,128]{1,0:T(8,128)S(1)}, u32[]{:S(2)}, u32[]{:S(2)}) %collective-permute-start.7) | collective-permute-done | bytes 262176 | tf_op jit(solution)/shard_map/ppermute | solution.py:222
  10.2 0.9 %copy-done = f32[512,128]{1,0:T(8,128)S(1)} copy-done((f32[512,128]{1,0:T(8,128)S(1)}, f32[512,128]{1,0:T(8,128)}, u32[]{:S(2)}) %copy-start) | copy-done | bytes 262168
  11.1 0.4 own.1
  11.6 0.0 collective-permute-done.mate_ref
  11.6 0.4 mate.1
  12.0 2.3 %near.1 = (f32[128,512]{1,0:T(8,128)S(1)}, f32[512,512]{1,0:T(8,128)S(1)}, f32[512,512]{1,0:T(8,128)S(1)}, f32[512,512]{1,0:T(8,128)S(1)}, f32[512,512]{1,0:T(8,128)S(1)}) custom-call(bf16[512,256]{1,0:T(8,128)(2,1)S(1)} %get-tuple-element.29.own_ref.refs_0_, bf16[512,256]{1,0:T(8,128)(2,1)S(1)} %get-tuple-element.30.mate_ref.refs_1_, f32[2048,512]{1,0:T(8,128)} %trailing_ref.1), custom_call_target="tpu_custom_call" | custom-call | tf_op jit(solution)/shard_map/near/pallas_call | solution.py:264
  14.3 0.5 far.1
  14.8 0.0 collective-permute-done.8.piece_ref
  14.8 0.5 %last.1 = (bf16[512,256]{1,0:T(8,128)(2,1)S(1)}, f32[128,128]{1,0:T(8,128)S(1)}, f32[128,128]{1,0:T(8,128)S(1)}, f32[128,128]{1,0:T(8,128)S(1)}, f32[128,128]{1,0:T(8,128)S(1)}) custom-call(f32[512,128]{1,0:T(8,128)S(1)} %collective-permute-done.8.piece_ref, f32[512,512]{1,0:T(8,128)S(1)} %get-tuple-element.34.held_ref.refs_3_, ...), custom_call_target="tpu_custom_call" | custom-call | tf_op jit(solution)/shard_map/last/pallas_call | solution.py:278
  15.3 1.8 %collective-permute-start.9 = (f32[128,128]{1,0:T(8,128)S(1)}, f32[128,128]{1,0:T(8,128)S(1)}, u32[]{:S(2)}, u32[]{:S(2)}) collective-permute-start(f32[128,128]{1,0:T(8,128)S(1)} %get-tuple-element.40), channel_id=1, source_target_pairs={{0,4},{4,0},{8,12},{12,8},{16,20},{20,16},{24,28},{28,24},{1,5},{5... | collective-permute-start | bytes 196616 | tf_op jit(solution)/shard_map/ppermute | solution.py:222
  17.1 1.6 %collective-permute-start.10 = (f32[128,128]{1,0:T(8,128)S(1)}, f32[128,128]{1,0:T(8,128)S(1)}, u32[]{:S(2)}, u32[]{:S(2)}) collective-permute-start(f32[128,128]{1,0:T(8,128)S(1)} %get-tuple-element.41), channel_id=1, source_target_pairs={{0,8},{4,12},{8,0},{12,4},{16,24},{20,28},{24,16},{28,20},{1,9},{5... | collective-permute-start | bytes 196616 | tf_op jit(solution)/shard_map/ppermute | solution.py:222
  18.7 0.1 collective-permute-start.11
  18.8 2.8 %collective-permute-start.3 = (f32[64,128]{1,0:T(8,128)S(1)}, f32[64,128]{1,0:T(8,128)S(1)}, u32[]{:S(2)}, u32[]{:S(2)}) collective-permute-start(f32[64,128]{1,0:T(8,128)S(1)} %get-tuple-element.26), channel_id=1, source_target_pairs={{0,12},{4,8},{8,4},{12,0},{16,28},{20,24},{24,20},{28,16},{1,13},{... | collective-permute-start | bytes 98312 | tf_op jit(solution)/shard_map/ppermute | solution.py:222
  21.6 0.4 collective-permute-start.2
  22.1 0.0 collective-permute-done.9
  22.1 0.2 collective-permute-start.1
  22.3 1.9 %collective-permute-done.11 = f32[128,128]{1,0:T(8,128)S(1)} collective-permute-done((f32[128,128]{1,0:T(8,128)S(1)}, f32[128,128]{1,0:T(8,128)S(1)}, u32[]{:S(2)}, u32[]{:S(2)}) %collective-permute-start.11) | collective-permute-done | bytes 65568 | tf_op jit(solution)/shard_map/ppermute | solution.py:222
  24.3 2.7 %collective-permute-start.12 = (f32[128,128]{1,0:T(8,128)S(1)}, f32[128,128]{1,0:T(8,128)S(1)}, u32[]{:S(2)}, u32[]{:S(2)}) collective-permute-start(f32[128,128]{1,0:T(8,128)S(1)} %add_add_fusion), channel_id=1, source_target_pairs={{0,16},{4,20},{8,24},{12,28},{16,0},{20,4},{24,8},{28,12},{1,17},{... | collective-permute-start | bytes 196616 | tf_op jit(solution)/shard_map/ppermute | solution.py:222
  27.0 1.7 %collective-permute-start.4 = (f32[64,128]{1,0:T(8,128)S(1)}, f32[64,128]{1,0:T(8,128)S(1)}, u32[]{:S(2)}, u32[]{:S(2)}) collective-permute-start(f32[64,128]{1,0:T(8,128)S(1)} %add_add_fusion.1), channel_id=1, source_target_pairs={{0,16},{4,20},{8,24},{12,28},{16,0},{20,4},{24,8},{28,12},{1,17},{... | collective-permute-start | bytes 98312 | tf_op jit(solution)/shard_map/ppermute | solution.py:222
  28.7 3.5 %collective-permute-done.4 = f32[64,128]{1,0:T(8,128)S(1)} collective-permute-done((f32[64,128]{1,0:T(8,128)S(1)}, f32[64,128]{1,0:T(8,128)S(1)}, u32[]{:S(2)}, u32[]{:S(2)}) %collective-permute-start.4) | collective-permute-done | bytes 32800 | tf_op jit(solution)/shard_map/ppermute | solution.py:222
  32.2 1.5 %collective-permute-start.5 = (f32[64,128]{1,0:T(8,128)S(1)}, f32[64,128]{1,0:T(8,128)S(1)}, u32[]{:S(2)}, u32[]{:S(2)}) collective-permute-start(f32[64,128]{1,0:T(8,128)S(1)} %add.30), channel_id=1, source_target_pairs={{0,2},{1,3},{2,0},{3,1},{4,6},{5,7},{6,4},{7,5},{8,10},{9,11},{10,... | collective-permute-start | bytes 98312 | tf_op jit(solution)/shard_map/ppermute | solution.py:222
  33.7 1.1 %collective-permute-start.15 = (f32[128,128]{1,0:T(8,128)S(1)}, f32[128,128]{1,0:T(8,128)S(1)}, u32[]{:S(2)}, u32[]{:S(2)}) collective-permute-start(f32[128,128]{1,0:T(8,128)S(1)} %add.35.refs_4_), channel_id=1, source_target_pairs={{0,12},{4,8},{8,4},{12,0},{16,28},{20,24},{24,20},{28,16},{1,13},{... | collective-permute-start | bytes 196616 | tf_op jit(solution)/shard_map/ppermute | solution.py:222
  34.8 0.6 %collective-permute-start.14 = (f32[128,128]{1,0:T(8,128)S(1)}, f32[128,128]{1,0:T(8,128)S(1)}, u32[]{:S(2)}, u32[]{:S(2)}) collective-permute-start(f32[128,128]{1,0:T(8,128)S(1)} %add.35.refs_4_), channel_id=1, source_target_pairs={{0,8},{4,12},{8,0},{12,4},{16,24},{20,28},{24,16},{28,20},{1,9},{5... | collective-permute-start | bytes 196616 | tf_op jit(solution)/shard_map/ppermute | solution.py:222
  35.4 1.9 %collective-permute-start.13 = (f32[128,128]{1,0:T(8,128)S(1)}, f32[128,128]{1,0:T(8,128)S(1)}, u32[]{:S(2)}, u32[]{:S(2)}) collective-permute-start(f32[128,128]{1,0:T(8,128)S(1)} %add.35.refs_4_), channel_id=1, source_target_pairs={{0,4},{4,0},{8,12},{12,8},{16,20},{20,16},{24,28},{28,24},{1,5},{5... | collective-permute-start | bytes 196616 | tf_op jit(solution)/shard_map/ppermute | solution.py:222
  37.3 0.1 collective-permute-start.6
  37.3 1.2 %collective-permute-done.6.other_ref = f32[64,128]{1,0:T(8,128)S(1)} collective-permute-done((f32[64,128]{1,0:T(8,128)S(1)}, f32[64,128]{1,0:T(8,128)S(1)}, u32[]{:S(2)}, u32[]{:S(2)}) %collective-permute-start.6) | collective-permute-done | bytes 32800 | tf_op jit(solution)/shard_map/ppermute | solution.py:222
  38.5 4.6 %factor.1 = (f32[128,128]{1,0:T(8,128)}, bf16[256,256]{1,0:T(8,128)(2,1)S(1)}) custom-call(f32[64,128]{1,0:T(8,128)S(1)} %add.31.mine_ref, f32[64,128]{1,0:T(8,128)S(1)} %collective-permute-done.6.other_ref), custom_call_target="tpu_custom_call" | custom-call | tf_op jit(solution)/shard_map/factor/pallas_call | solution.py:291
  43.1 0.6 %basis.1.basis_ref = bf16[2048,256]{1,0:T(8,128)(2,1)S(1)} custom-call(bf16[256,256]{1,0:T(8,128)(2,1)S(1)} %get-tuple-element.28.solve_ref, bf16[512,256]{1,0:T(8,128)(2,1)S(1)} %get-tuple-element.29.own_ref.refs_0_, bf16[512,256]{1,0:T(8,128)(2,1)S(1)} %get-tuple-element.30.mate_ref.refs_1_, bf16[512,256]{1,0:T(8,128)(2,1)S(1)} %get-tuple-element.33.refs_2_, ...), custom_call_target="tpu_custom_call" | custom-call | tf_op jit(solution)/shard_map/basis/pallas_call | solution.py:303
  43.7 1.7 %shard_map.49 = (f32[128,512]{1,0:T(8,128)S(1)}, f32[2048,512]{1,0:T(8,128)}) custom-call(bf16[256,256]{1,0:T(8,128)(2,1)S(1)} %get-tuple-element.28.solve_ref, bf16[2048,256]{1,0:T(8,128)(2,1)S(1)} %basis.1.basis_ref, f32[512,512]{1,0:T(8,128)S(1)} %get-tuple-element.37.refs_0_, f32[512,512]{1,0:T(8,128)S(1)} %get-tuple-element.38.refs_1_, ...), custom_call_target="tpu_custom_call" | custom-call | tf_op jit(solution)/shard_map/pallas_call | solution.py:311
  45.5 2.4 %shard_map.50 = (f32[128,512]{1,0:T(8,128)}, f32[2048,512]{1,0:T(8,128)}) custom-call(bf16[256,256]{1,0:T(8,128)(2,1)S(1)} %get-tuple-element.28.solve_ref, bf16[2048,256]{1,0:T(8,128)(2,1)S(1)} %basis.1.basis_ref, f32[512,512]{1,0:T(8,128)S(1)} %get-tuple-element.37.refs_0_, ...), custom_call_target="tpu_custom_call", output_to_operand_aliasing={{1}: (9, {})} | custom-call | tf_op jit(solution)/shard_map/pallas_call | solution.py:311
  (16 shorter events, 0.1 us)
Async XLA Ops:
  0.6 9.5 %collective-permute-start.7 = (f32[512,128]{1,0:T(8,128)}, f32[512,128]{1,0:T(8,128)S(1)}, u32[]{:S(2)}, u32[]{:S(2)}) collective-permute-start(f32[512,128]{1,0:T(8,128)} %panel_ref.1), channel_id=1, source_target_pairs={{0,2},{1,3},{2,0},{3,1},{4,6},{5,7},{6,4},{7,5},{8,10},{9,11},{10,... | collective-permute-start | bytes 786440 | tf_op jit(solution)/shard_map/ppermute | solution.py:222
  3.7 7.9 %collective-permute-start = (f32[512,128]{1,0:T(8,128)}, f32[512,128]{1,0:T(8,128)S(1)}, u32[]{:S(2)}, u32[]{:S(2)}) collective-permute-start(f32[512,128]{1,0:T(8,128)} %panel_ref.1), channel_id=1, source_target_pairs={{0,1},{1,0},{2,3},{3,2},{4,5},{5,4},{6,7},{7,6},{8,9},{9,8},{10,11... | collective-permute-start | bytes 786440 | tf_op jit(solution)/shard_map/ppermute | solution.py:222
  10.2 4.6 %collective-permute-start.8 = (f32[512,128]{1,0:T(8,128)S(1)}, f32[512,128]{1,0:T(8,128)S(1)}, u32[]{:S(2)}, u32[]{:S(2)}) collective-permute-start(f32[512,128]{1,0:T(8,128)S(1)} %collective-permute-done.7.piece_ref), channel_id=1, source_target_pairs={{0,1},{1,0},{2,3},{3,2},{4,5},{5,4},{6,7},{7,6},{8,9},{9,8},{10,11... | collective-permute-start | bytes 786440 | tf_op jit(solution)/shard_map/ppermute | solution.py:222
  10.2 1.0 %copy-start = (f32[512,128]{1,0:T(8,128)S(1)}, f32[512,128]{1,0:T(8,128)}, u32[]{:S(2)}) copy-start(f32[512,128]{1,0:T(8,128)} %panel_ref.1) | copy-start | bytes 786436
  15.3 6.8 %collective-permute-start.9 = (f32[128,128]{1,0:T(8,128)S(1)}, f32[128,128]{1,0:T(8,128)S(1)}, u32[]{:S(2)}, u32[]{:S(2)}) collective-permute-start(f32[128,128]{1,0:T(8,128)S(1)} %get-tuple-element.40), channel_id=1, source_target_pairs={{0,4},{4,0},{8,12},{12,8},{16,20},{20,16},{24,28},{28,24},{1,5},{5... | collective-permute-start | bytes 196616 | tf_op jit(solution)/shard_map/ppermute | solution.py:222
  17.1 5.2 %collective-permute-start.10 = (f32[128,128]{1,0:T(8,128)S(1)}, f32[128,128]{1,0:T(8,128)S(1)}, u32[]{:S(2)}, u32[]{:S(2)}) collective-permute-start(f32[128,128]{1,0:T(8,128)S(1)} %get-tuple-element.41), channel_id=1, source_target_pairs={{0,8},{4,12},{8,0},{12,4},{16,24},{20,28},{24,16},{28,20},{1,9},{5... | collective-permute-start | bytes 196616 | tf_op jit(solution)/shard_map/ppermute | solution.py:222
  18.7 5.5 %collective-permute-start.11 = (f32[128,128]{1,0:T(8,128)S(1)}, f32[128,128]{1,0:T(8,128)S(1)}, u32[]{:S(2)}, u32[]{:S(2)}) collective-permute-start(f32[128,128]{1,0:T(8,128)S(1)} %get-tuple-element.42), channel_id=1, source_target_pairs={{0,12},{4,8},{8,4},{12,0},{16,28},{20,24},{24,20},{28,16},{1,13},{... | collective-permute-start | bytes 196616 | tf_op jit(solution)/shard_map/ppermute | solution.py:222
  18.8 8.1 %collective-permute-start.3 = (f32[64,128]{1,0:T(8,128)S(1)}, f32[64,128]{1,0:T(8,128)S(1)}, u32[]{:S(2)}, u32[]{:S(2)}) collective-permute-start(f32[64,128]{1,0:T(8,128)S(1)} %get-tuple-element.26), channel_id=1, source_target_pairs={{0,12},{4,8},{8,4},{12,0},{16,28},{20,24},{24,20},{28,16},{1,13},{... | collective-permute-start | bytes 98312 | tf_op jit(solution)/shard_map/ppermute | solution.py:222
  21.6 5.3 %collective-permute-start.2 = (f32[64,128]{1,0:T(8,128)S(1)}, f32[64,128]{1,0:T(8,128)S(1)}, u32[]{:S(2)}, u32[]{:S(2)}) collective-permute-start(f32[64,128]{1,0:T(8,128)S(1)} %get-tuple-element.26), channel_id=1, source_target_pairs={{0,8},{4,12},{8,0},{12,4},{16,24},{20,28},{24,16},{28,20},{1,9},{5... | collective-permute-start | bytes 98312 | tf_op jit(solution)/shard_map/ppermute | solution.py:222
  22.1 4.9 %collective-permute-start.1 = (f32[64,128]{1,0:T(8,128)S(1)}, f32[64,128]{1,0:T(8,128)S(1)}, u32[]{:S(2)}, u32[]{:S(2)}) collective-permute-start(f32[64,128]{1,0:T(8,128)S(1)} %get-tuple-element.26), channel_id=1, source_target_pairs={{0,4},{4,0},{8,12},{12,8},{16,20},{20,16},{24,28},{28,24},{1,5},{5... | collective-permute-start | bytes 98312 | tf_op jit(solution)/shard_map/ppermute | solution.py:222
  24.3 9.4 %collective-permute-start.12 = (f32[128,128]{1,0:T(8,128)S(1)}, f32[128,128]{1,0:T(8,128)S(1)}, u32[]{:S(2)}, u32[]{:S(2)}) collective-permute-start(f32[128,128]{1,0:T(8,128)S(1)} %add_add_fusion), channel_id=1, source_target_pairs={{0,16},{4,20},{8,24},{12,28},{16,0},{20,4},{24,8},{28,12},{1,17},{... | collective-permute-start | bytes 196616 | tf_op jit(solution)/shard_map/ppermute | solution.py:222
  27.0 5.2 %collective-permute-start.4 = (f32[64,128]{1,0:T(8,128)S(1)}, f32[64,128]{1,0:T(8,128)S(1)}, u32[]{:S(2)}, u32[]{:S(2)}) collective-permute-start(f32[64,128]{1,0:T(8,128)S(1)} %add_add_fusion.1), channel_id=1, source_target_pairs={{0,16},{4,20},{8,24},{12,28},{16,0},{20,4},{24,8},{28,12},{1,17},{... | collective-permute-start | bytes 98312 | tf_op jit(solution)/shard_map/ppermute | solution.py:222
  32.2 5.1 %collective-permute-start.5 = (f32[64,128]{1,0:T(8,128)S(1)}, f32[64,128]{1,0:T(8,128)S(1)}, u32[]{:S(2)}, u32[]{:S(2)}) collective-permute-start(f32[64,128]{1,0:T(8,128)S(1)} %add.30), channel_id=1, source_target_pairs={{0,2},{1,3},{2,0},{3,1},{4,6},{5,7},{6,4},{7,5},{8,10},{9,11},{10,... | collective-permute-start | bytes 98312 | tf_op jit(solution)/shard_map/ppermute | solution.py:222
  33.7 10.0 %collective-permute-start.15 = (f32[128,128]{1,0:T(8,128)S(1)}, f32[128,128]{1,0:T(8,128)S(1)}, u32[]{:S(2)}, u32[]{:S(2)}) collective-permute-start(f32[128,128]{1,0:T(8,128)S(1)} %add.35.refs_4_), channel_id=1, source_target_pairs={{0,12},{4,8},{8,4},{12,0},{16,28},{20,24},{24,20},{28,16},{1,13},{... | collective-permute-start | bytes 196616 | tf_op jit(solution)/shard_map/ppermute | solution.py:222
  34.8 10.6 %collective-permute-start.14 = (f32[128,128]{1,0:T(8,128)S(1)}, f32[128,128]{1,0:T(8,128)S(1)}, u32[]{:S(2)}, u32[]{:S(2)}) collective-permute-start(f32[128,128]{1,0:T(8,128)S(1)} %add.35.refs_4_), channel_id=1, source_target_pairs={{0,8},{4,12},{8,0},{12,4},{16,24},{20,28},{24,16},{28,20},{1,9},{5... | collective-permute-start | bytes 196616 | tf_op jit(solution)/shard_map/ppermute | solution.py:222
  35.4 10.1 %collective-permute-start.13 = (f32[128,128]{1,0:T(8,128)S(1)}, f32[128,128]{1,0:T(8,128)S(1)}, u32[]{:S(2)}, u32[]{:S(2)}) collective-permute-start(f32[128,128]{1,0:T(8,128)S(1)} %add.35.refs_4_), channel_id=1, source_target_pairs={{0,4},{4,0},{8,12},{12,8},{16,20},{20,16},{24,28},{28,24},{1,5},{5... | collective-permute-start | bytes 196616 | tf_op jit(solution)/shard_map/ppermute | solution.py:222
  37.3 1.3 %collective-permute-start.6 = (f32[64,128]{1,0:T(8,128)S(1)}, f32[64,128]{1,0:T(8,128)S(1)}, u32[]{:S(2)}, u32[]{:S(2)}) collective-permute-start(f32[64,128]{1,0:T(8,128)S(1)} %add.31.mine_ref), channel_id=1, source_target_pairs={{0,1},{1,0},{2,3},{3,2},{4,5},{5,4},{6,7},{7,6},{8,9},{9,8},{10,11... | collective-permute-start | bytes 98312 | tf_op jit(solution)/shard_map/ppermute | solution.py:222

commit v3 on v2

v3 whole, which is shorter than its diff:
```python
import functools
import math

import jax
import jax.numpy as jnp
from jax import lax
from jax.experimental import pallas as pl
from jax.experimental.pallas import tpu as pltpu
from jax.sharding import PartitionSpec as P


HIGHEST = lax.Precision.HIGHEST
CUTS = 2
BLOCK, STEP = 32, 16
COST = pl.CostEstimate(flops=1 << 31, bytes_accessed=1 << 23, transcendentals=0)
CHUNK = 128
VMEM = pl.BlockSpec(memory_space=pltpu.VMEM)
HBM = pl.BlockSpec(memory_space=pltpu.HBM)


def limit(mebibytes):
    return pltpu.CompilerParams(vmem_limit_bytes=mebibytes << 20)


def f32(*shape):
    return jax.ShapeDtypeStruct(shape, jnp.float32)


def split(value):
    high = value.astype(jnp.bfloat16)
    return high, (value - high.astype(jnp.float32)).astype(jnp.bfloat16)


def store_split(split_ref, piece):
    width = piece.shape[1]
    split_ref[:, :width], split_ref[:, width:] = split(piece)


def cross_of(split_ref, block):
    width = split_ref.shape[1] // 2
    high, low = split_ref[:, :width], split_ref[:, width:]
    block_high, block_low = split(block)
    contract = ((0,), (0,))
    product = dot(high, block_high, contract)
    return product + dot(high, block_low, contract) + dot(low, block_high, contract)


def dot(first, second, dims, precision=None):
    return lax.dot_general(
        first, second, (dims, ((), ())), precision=precision, preferred_element_type=jnp.float32
    )


def block_of(offset, rows):
    return (lax.axis_index("col") ^ offset) * rows


def part_of(offset, group):
    return (lax.axis_index("row") & (group - 1)) ^ offset


def wait_all(copies):
    for copy in copies:
        copy.wait()


def own_kernel(panel_ref, gram_ref, split_ref):
    panel = panel_ref[...]
    gram_ref[...] = dot(panel, panel, ((0,), (0,)), HIGHEST)
    store_split(split_ref, panel)


def mate_kernel(mate_ref, gram_in_ref, gram_ref, split_ref, sum_ref, *, near):
    mate = mate_ref[...]
    half = mate.shape[1] // 2
    sum_ref[...] = gram_in_ref[...] + dot(mate, mate, ((0,), (0,)), HIGHEST)
    upper = jnp.where((lax.axis_index("col") & near) == 0, 0, half)
    gram_ref[...] = sum_ref[pl.ds(pl.multiple_of(upper, half), half), :]
    store_split(split_ref, mate)


def rows_of(held_ref, offset, rows):
    return held_ref[pl.ds(pl.multiple_of(block_of(offset, rows), rows), rows), :]


def near_kernel(own_ref, mate_ref, held_ref, cross_ref, *, order):
    rows = own_ref.shape[0]
    total = cross_of(own_ref, rows_of(held_ref, order[0], rows))
    cross_ref[...] = total + cross_of(mate_ref, rows_of(held_ref, order[1], rows))


def far_kernel(piece_ref, held_ref, cross_in_ref, split_ref, cross_ref, *, offset):
    store_split(split_ref, piece_ref[...])
    block = rows_of(held_ref, offset, piece_ref.shape[0])
    cross_ref[...] = cross_in_ref[...] + cross_of(split_ref, block)


def last_kernel(piece_ref, held_ref, cross_in_ref, split_ref, *refs, offset):
    *part_refs, sum_ref = refs
    store_split(split_ref, piece_ref[...])
    block = rows_of(held_ref, offset, piece_ref.shape[0])
    sum_ref[...] = cross_in_ref[...] + cross_of(split_ref, block)
    part = part_refs[0].shape[1]
    for k, part_ref in enumerate(part_refs):
        first = pl.multiple_of(part_of(k, len(part_refs)) * part, part)
        part_ref[...] = sum_ref[:, pl.ds(first, part)]


def factor_kernel(*refs, near, block, step, norm_scale):
    *half_refs, scaled_ref, solve_ref = refs
    width = scaled_ref.shape[1]
    first_half = (lax.axis_index("col") & near) == 0
    mine, other = (sum(ref[...] for ref in half_refs[k::2]) for k in range(2))
    gram = jnp.concatenate(
        [jnp.where(first_half, mine, other), jnp.where(first_half, other, mine)], 0
    )
    local = lax.broadcasted_iota(jnp.int32, (step, 1), 0)
    lanes = lax.broadcasted_iota(jnp.int32, (block, width), 1)
    rows = lax.broadcasted_iota(jnp.int32, (block, width), 0)
    factor_rows, inverse_rows = [], []
    for first in range(0, width, block):
        left = gram[first : first + block, :]
        right = jnp.where(lanes == rows + first, 1.0, 0.0)
        if factor_rows:
            above = jnp.concatenate(factor_rows, 0)
            both = jnp.concatenate([above, jnp.concatenate(inverse_rows, 0)], 1)
            update = dot(above[:, first : first + block], both, ((0,), (0,)), HIGHEST)
            left = left - update[:, :width]
            right = right - update[:, width:]
        left_done, right_done = [], []
        for start in range(first, first + block, step):
            columns = [
                jnp.broadcast_to(left[:, start + j : start + j + 1], left.shape) for j in range(step)
            ]
            pivots = jnp.ones((step, width), jnp.float32)
            for k in range(step):
                pivot = columns[k][k : k + 1, :]
                pivots = jnp.where(local == k, pivot, pivots)
                ratio = columns[k] * (1.0 / pivot)
                for j in range(k + 1, step):
                    columns[j] = columns[j] - ratio * columns[j][k : k + 1, :]
                head = jnp.where(local > k, ratio[:step], 0.0)
                if ratio.shape[0] > step:
                    head = jnp.concatenate([head, ratio[step:]], 0)
                ratio = head
                left = left - ratio * left[k : k + 1, :]
                right = right - ratio * right[k : k + 1, :]
            scale = lax.rsqrt(pivots)
            left_done.append(left[:step] * scale)
            right_done.append(right[:step] * scale)
            left, right = left[step:], right[step:]
        factor_rows.append(jnp.where(lanes >= rows + first, jnp.concatenate(left_done, 0), 0.0))
        inverse_rows.append(jnp.where(lanes <= rows + first, jnp.concatenate(right_done, 0), 0.0))
        scaled_ref[first : first + block, :] = factor_rows[-1] * norm_scale
    inverse = jnp.concatenate(inverse_rows, 0)
    solve = jnp.concatenate([inverse, dot(inverse, inverse, ((0,), (0,)), HIGHEST)], 0)
    store_split(solve_ref, solve)


def final_kernel(solve_ref, held_ref, *refs, order, group, norm_scale, chunk):
    split_refs, refs = refs[: len(order)], refs[len(order) :]
    part_refs, (w_ref, remainder_ref, cross_ref, w_here, result, w_sem, sems) = refs[:group], refs[group:]
    width, part = part_refs[0].shape
    for k, part_ref in enumerate(part_refs):
        cross_ref[:, pl.ds(pl.multiple_of(part_of(k, group) * part, part), part)] = part_ref[...]
    contract = ((1,), (0,))
    high, low = split(cross_ref[...])
    both = solve_ref[...]
    solved = dot(
        jnp.concatenate([both, both[:, :width]], 1), jnp.concatenate([high, high, low], 0), contract
    )
    w_here[...] = solved[:width] * norm_scale
    w_copy = pltpu.make_async_copy(w_here, w_ref, w_sem)
    w_copy.start()
    high, low = split(solved[width:])
    right = jnp.concatenate([high, high, low], 0)
    copies = [w_copy]
    rows = split_refs[0].shape[0]
    cuts = sems.shape[1]
    for i, split_ref in enumerate(split_refs):
        base = pl.multiple_of(block_of(order[i], rows), rows)
        for first in range(0, rows, chunk):
            both = split_ref[first : first + chunk, :]
            product = dot(jnp.concatenate([both, both[:, :width]], 1), right, contract)
            held = held_ref[pl.ds(pl.multiple_of(base + first, chunk), chunk), :]
            result[i, first : first + chunk, :] = held - product
            done = first + chunk
            if done % (rows // cuts) == 0:
                n = done * cuts // rows - 1
                here = pl.ds(n * (rows // cuts), rows // cuts)
                there = pl.ds(pl.multiple_of(base + n * (rows // cuts), rows // cuts), rows // cuts)
                copies.append(
                    pltpu.make_async_copy(result.at[i, here], remainder_ref.at[there], sems.at[i, n])
                )
                copies[-1].start()
    wait_all(copies)


def swap(value, axis, bit):
    size = lax.axis_size(axis)
    return lax.ppermute(value, axis, [(i, i ^ bit) for i in range(size)])


def bits_of(axis):
    size = lax.axis_size(axis)
    assert size & (size - 1) == 0
    return [1 << b for b in range(size.bit_length() - 1)]


def body(panel_block, trailing):
    row_bits, col_bits = bits_of("row"), bits_of("col")
    near, far_bits = col_bits[0], col_bits[1:]
    piece_rows, width = panel_block.shape
    trailing_rows, columns = trailing.shape
    group_bits = row_bits[:2]
    group = 1 << len(group_bits)
    part = columns // group
    total_rows = trailing_rows * lax.axis_size("row")
    norm_scale = 1.0 / math.sqrt(total_rows)

    far, offsets = [panel_block], [0]
    for bit in far_bits:
        far = far + [swap(piece, "col", bit) for piece in far]
        offsets = offsets + [o ^ bit for o in offsets]
    mate = swap(panel_block, "col", near)
    last = [swap(piece, "col", near) for piece in far[1:]]
    order = [0, near] + offsets[1:] + [o ^ near for o in offsets[1:]]

    square, wide = f32(width, width), f32(width, columns)
    half_square = f32(width // 2, width)
    split_shape = jax.ShapeDtypeStruct((piece_rows, 2 * width), jnp.bfloat16)
    copies = pltpu.SemaphoreType.DMA
    gram, own_split = pl.pallas_call(
        own_kernel, out_shape=(square, split_shape), in_specs=[VMEM], out_specs=(VMEM,) * 2,
        compiler_params=limit(8), name="own", cost_estimate=COST,
    )(pltpu.with_memory_space_constraint(panel_block, pltpu.HBM))
    gram, mate_split = pl.pallas_call(
        functools.partial(mate_kernel, near=near),
        out_shape=(half_square, split_shape), in_specs=[VMEM] * 2, out_specs=(VMEM,) * 2,
        scratch_shapes=[pltpu.VMEM((width, width), jnp.float32)],
        compiler_params=limit(8), name="mate", cost_estimate=COST,
    )(mate, gram)
    held = pltpu.with_memory_space_constraint(trailing, pltpu.VMEM)
    cross = pl.pallas_call(
        functools.partial(near_kernel, order=order), out_shape=wide,
        in_specs=[VMEM] * 3, out_specs=VMEM, compiler_params=limit(16), name="near",
    )(own_split, mate_split, held)
    splits = [own_split, mate_split]
    pieces = far[1:] + last
    for i, piece in enumerate(pieces[:-1]):
        split_out, cross = pl.pallas_call(
            functools.partial(far_kernel, offset=order[i + 2]),
            out_shape=(split_shape, wide), in_specs=[VMEM] * 3,
            out_specs=(VMEM,) * 2, compiler_params=limit(16), name="far",
        )(piece, held, cross)
        splits.append(split_out)
    split_out, *parts = pl.pallas_call(
        functools.partial(last_kernel, offset=order[-1]),
        out_shape=(split_shape,) + (f32(width, part),) * group,
        in_specs=[VMEM] * 3, out_specs=(VMEM,) * (1 + group),
        scratch_shapes=[pltpu.VMEM((width, columns), jnp.float32)],
        compiler_params=limit(16), name="last",
    )(pieces[-1], held, cross)
    splits.append(split_out)

    gram = gram + sum(swap(gram, "row", k) for k in range(1, group))
    for bit in row_bits[len(group_bits) :]:
        gram = gram + swap(gram, "row", bit)
    halves = [gram if o == 0 else swap(gram, "col", o) for f in offsets for o in (f, f ^ near)]
    r_scaled, solve = pl.pallas_call(
        functools.partial(factor_kernel, near=near, block=BLOCK, step=STEP, norm_scale=norm_scale),
        out_shape=(square, jax.ShapeDtypeStruct((2 * width, 2 * width), jnp.bfloat16)),
        in_specs=[VMEM] * len(halves), out_specs=(VMEM, VMEM), compiler_params=limit(4), name="factor",
    )(*halves)
    mine = parts[0]
    for k in range(1, group):
        mine = mine + swap(parts[k], "row", k)
    for bit in row_bits[len(group_bits) :]:
        mine = mine + swap(mine, "row", bit)
    others = [swap(mine, "row", k) for k in range(1, group)]

    w_scaled, remainder = pl.pallas_call(
        functools.partial(final_kernel, order=order, group=group, norm_scale=norm_scale, chunk=CHUNK),
        out_shape=(wide, f32(trailing_rows, columns)),
        in_specs=[VMEM] * (2 + len(order) + group), out_specs=(HBM, HBM),
        scratch_shapes=[
            pltpu.VMEM((width, columns), jnp.float32),
            pltpu.VMEM((width, columns), jnp.float32),
            pltpu.VMEM((len(order), piece_rows, columns), jnp.float32),
            copies,
            copies((len(order), CUTS)),
        ],
        compiler_params=limit(20), name="final",
    )(solve, held, *splits, mine, *others)
    return r_scaled, w_scaled, remainder


def solution(mesh):
    in_specs = (P(("row", "col"), None), P("row", "col"))
    out_specs = (P(), P(None, "col"), P("row", "col"))

    return jax.shard_map(body, mesh=mesh, in_specs=in_specs, out_specs=out_specs, check_vma=False)
```

time: 48 us -> 46.9 us (0.977)
  Pallas kernels: 13.4 us -> 10.1 us
  waiting for transfers between devices: 13.2 us -> 14.5 us
  local copies, waits for them, and re-layouts: 0.95 us -> 1.74 us
    pallas_call x7 -> x5, Pallas kernels: 12.6 us -> 8.34 us  [the longest x1 3.93 us: body(): pl.pallas_call(functools.partial(factor_kernel, near=near, block=BLOCK, s...]
    ppermute x16 -> x17, waiting for transfers between devices: 13.2 us -> 14.5 us  [swap(): return lax.ppermute(value, axis, [(i, i ^ bit) for i in range(size)])]
    pallas_call x1, Pallas kernels: 0.41 us -> 1.37 us  [body(): pl.pallas_call(own_kernel, out_shape=(square, split_shape), in_specs=[VME...]
    unnamed x2, local copies, waits for them, and re-layouts: 0.95 us -> 1.74 us
    ppermute x16 -> x17, starting transfers between devices: 19.5 us -> 19.5 us  [swap(): return lax.ppermute(value, axis, [(i, i ^ bit) for i in range(size)])]
  transfers between devices with their start and end apart: 16 -> 17, of which waited for: 4 -> 4; matrix products, arithmetic and copies ran while one was open for 0% -> 0% of each run, Pallas kernels for 22% -> 15%
where the time goes in v3:
time: 46.9 us; the launch traced here: 46.7 us
  starting transfers between devices  19.5 us (42%)
  waiting for transfers between devices  14.5 us (31%)
  Pallas kernels  10.1 us (22%)
  local copies, waits for them, and re-layouts  1.74 us (4%)
  between operations  0.74 us (2%)
    ppermute x17, starting transfers between devices, swap(): return lax.ppermute(value, axis, [(i, i ^ bit) for i in range(size)])  19.5 us
    ppermute x17, waiting for transfers between devices, swap(): return lax.ppermute(value, axis, [(i, i ^ bit) for i in range(size)])  14.5 us
    pallas_call x1, Pallas kernels, body(): pl.pallas_call(functools.partial(factor_kernel, near=near, block=BLOCK, s...  3.93 us
    pallas_call x1, Pallas kernels, body(): pl.pallas_call(functools.partial(final_kernel, order=order, group=group,...  2.8 us
    unnamed x2, local copies, waits for them, and re-layouts  1.74 us
    pallas_call x1, Pallas kernels, body(): pl.pallas_call(own_kernel, out_shape=(square, split_shape), in_specs=[VME...  1.37 us
  transfers between devices with their start and end apart: 17, of which 4 were waited for; matrix products, arithmetic and copies ran while one was open for 0% of the time, Pallas kernels for 15%

profile of v3, /device:TPU:0, one launch (start us, length us, event | category | flops | bytes accessed | tf_op | source)
XLA Modules:
  0.0 46.7 jit_solution(13127567756287046645)
XLA Ops:
  0.6 3.0 %collective-permute-start.8 = (f32[512,128]{1,0:T(8,128)}, f32[512,128]{1,0:T(8,128)S(1)}, u32[]{:S(2)}, u32[]{:S(2)}) collective-permute-start(f32[512,128]{1,0:T(8,128)} %panel_ref.1), channel_id=1, source_target_pairs={{0,2},{1,3},{2,0},{3,1},{4,6},{5,7},{6,4},{7,5},{8,10},{9,11},{10,... | collective-permute-start | bytes 786440 | tf_op jit(solution)/shard_map/ppermute | solution.py:201
  3.7 0.0 collective-permute-start
  3.7 6.5 %collective-permute-done.8.piece_ref = f32[512,128]{1,0:T(8,128)S(1)} collective-permute-done((f32[512,128]{1,0:T(8,128)}, f32[512,128]{1,0:T(8,128)S(1)}, u32[]{:S(2)}, u32[]{:S(2)}) %collective-permute-start.8) | collective-permute-done | bytes 262176 | tf_op jit(solution)/shard_map/ppermute | solution.py:201
  10.2 1.4 %own.1 = (f32[128,128]{1,0:T(8,128)S(1)}, bf16[512,256]{1,0:T(8,128)(2,1)S(1)}) custom-call(f32[512,128]{1,0:T(8,128)} %panel_ref.1), custom_call_target="tpu_custom_call" | custom-call | flops 2147483648 | bytes 8388608 | tf_op jit(solution)/shard_map/own/pallas_call | solution.py:233
  11.6 0.0 copy-start
  11.6 0.4 mate.1
  12.0 1.7 %copy-done = f32[2048,512]{1,0:T(8,128)S(1)} copy-done((f32[2048,512]{1,0:T(8,128)S(1)}, f32[2048,512]{1,0:T(8,128)}, u32[]{:S(2)}) %copy-start) | copy-done | bytes 4194328
  13.7 0.6 %near.1.cross_in_ref = f32[128,512]{1,0:T(8,128)S(1)} custom-call(bf16[512,256]{1,0:T(8,128)(2,1)S(1)} %get-tuple-element.22.own_ref.refs_0_, bf16[512,256]{1,0:T(8,128)(2,1)S(1)} %get-tuple-element.23.mate_ref.refs_1_, f32[2048,512]{1,0:T(8,128)S(1)} %copy-done), custom_call_target="tpu_custom_call" | custom-call | tf_op jit(solution)/shard_map/near/pallas_call | solution.py:244
  14.4 0.5 far.1
  14.9 0.0 collective-permute-done.9.piece_ref
  14.9 0.5 %last.1 = (bf16[512,256]{1,0:T(8,128)(2,1)S(1)}, f32[128,128]{1,0:T(8,128)S(1)}, f32[128,128]{1,0:T(8,128)S(1)}, f32[128,128]{1,0:T(8,128)S(1)}, f32[128,128]{1,0:T(8,128)S(1)}) custom-call(f32[512,128]{1,0:T(8,128)S(1)} %collective-permute-done.9.piece_ref, f32[2048,512]{1,0:T(8,128)S(1)} %copy-done, f32[128,512]{1,0:T(8,128)S(1)} %get-tuple-element.25.cross_in_ref), custom_call_target="tpu_custom_call" | custom-call | tf_op jit(solution)/shard_map/last/pallas_call | solution.py:257
  15.4 1.8 %collective-permute-start.10 = (f32[128,128]{1,0:T(8,128)S(1)}, f32[128,128]{1,0:T(8,128)S(1)}, u32[]{:S(2)}, u32[]{:S(2)}) collective-permute-start(f32[128,128]{1,0:T(8,128)S(1)} %get-tuple-element.28), channel_id=1, source_target_pairs={{0,4},{4,0},{8,12},{12,8},{16,20},{20,16},{24,28},{28,24},{1,5},{5... | collective-permute-start | bytes 196616 | tf_op jit(solution)/shard_map/ppermute | solution.py:201
  17.2 1.6 %collective-permute-start.11 = (f32[128,128]{1,0:T(8,128)S(1)}, f32[128,128]{1,0:T(8,128)S(1)}, u32[]{:S(2)}, u32[]{:S(2)}) collective-permute-start(f32[128,128]{1,0:T(8,128)S(1)} %get-tuple-element.29), channel_id=1, source_target_pairs={{0,8},{4,12},{8,0},{12,4},{16,24},{20,28},{24,16},{28,20},{1,9},{5... | collective-permute-start | bytes 196616 | tf_op jit(solution)/shard_map/ppermute | solution.py:201
  18.8 0.1 collective-permute-start.12
  19.0 2.8 %collective-permute-start.3 = (f32[64,128]{1,0:T(8,128)S(1)}, f32[64,128]{1,0:T(8,128)S(1)}, u32[]{:S(2)}, u32[]{:S(2)}) collective-permute-start(f32[64,128]{1,0:T(8,128)S(1)} %get-tuple-element.19), channel_id=1, source_target_pairs={{0,12},{4,8},{8,4},{12,0},{16,28},{20,24},{24,20},{28,16},{1,13},{... | collective-permute-start | bytes 98312 | tf_op jit(solution)/shard_map/ppermute | solution.py:201
  21.8 0.4 collective-permute-start.2
  22.2 0.0 collective-permute-done.10
  22.2 0.3 collective-permute-start.1
  22.5 1.9 %collective-permute-done.12 = f32[128,128]{1,0:T(8,128)S(1)} collective-permute-done((f32[128,128]{1,0:T(8,128)S(1)}, f32[128,128]{1,0:T(8,128)S(1)}, u32[]{:S(2)}, u32[]{:S(2)}) %collective-permute-start.12) | collective-permute-done | bytes 65568 | tf_op jit(solution)/shard_map/ppermute | solution.py:201
  24.4 2.6 %collective-permute-start.13 = (f32[128,128]{1,0:T(8,128)S(1)}, f32[128,128]{1,0:T(8,128)S(1)}, u32[]{:S(2)}, u32[]{:S(2)}) collective-permute-start(f32[128,128]{1,0:T(8,128)S(1)} %add_add_fusion), channel_id=1, source_target_pairs={{0,16},{4,20},{8,24},{12,28},{16,0},{20,4},{24,8},{28,12},{1,17},{... | collective-permute-start | bytes 196616 | tf_op jit(solution)/shard_map/ppermute | solution.py:201
  27.0 0.0 collective-permute-done.3
  27.0 0.0 collective-permute-done.2
  27.1 1.7 %collective-permute-start.4 = (f32[64,128]{1,0:T(8,128)S(1)}, f32[64,128]{1,0:T(8,128)S(1)}, u32[]{:S(2)}, u32[]{:S(2)}) collective-permute-start(f32[64,128]{1,0:T(8,128)S(1)} %add_add_fusion.1), channel_id=1, source_target_pairs={{0,16},{4,20},{8,24},{12,28},{16,0},{20,4},{24,8},{28,12},{1,17},{... | collective-permute-start | bytes 98312 | tf_op jit(solution)/shard_map/ppermute | solution.py:201
  28.8 3.5 %collective-permute-done.4 = f32[64,128]{1,0:T(8,128)S(1)} collective-permute-done((f32[64,128]{1,0:T(8,128)S(1)}, f32[64,128]{1,0:T(8,128)S(1)}, u32[]{:S(2)}, u32[]{:S(2)}) %collective-permute-start.4) | collective-permute-done | bytes 32800 | tf_op jit(solution)/shard_map/ppermute | solution.py:201
  32.3 0.0 collective-permute-done.13
  32.3 1.1 %collective-permute-start.16 = (f32[128,128]{1,0:T(8,128)S(1)}, f32[128,128]{1,0:T(8,128)S(1)}, u32[]{:S(2)}, u32[]{:S(2)}) collective-permute-start(f32[128,128]{1,0:T(8,128)S(1)} %add.31.refs_4_), channel_id=1, source_target_pairs={{0,12},{4,8},{8,4},{12,0},{16,28},{20,24},{24,20},{28,16},{1,13},{... | collective-permute-start | bytes 196616 | tf_op jit(solution)/shard_map/ppermute | solution.py:201
  33.5 0.6 %collective-permute-start.15 = (f32[128,128]{1,0:T(8,128)S(1)}, f32[128,128]{1,0:T(8,128)S(1)}, u32[]{:S(2)}, u32[]{:S(2)}) collective-permute-start(f32[128,128]{1,0:T(8,128)S(1)} %add.31.refs_4_), channel_id=1, source_target_pairs={{0,8},{4,12},{8,0},{12,4},{16,24},{20,28},{24,16},{28,20},{1,9},{5... | collective-permute-start | bytes 196616 | tf_op jit(solution)/shard_map/ppermute | solution.py:201
  34.0 1.9 %collective-permute-start.14 = (f32[128,128]{1,0:T(8,128)S(1)}, f32[128,128]{1,0:T(8,128)S(1)}, u32[]{:S(2)}, u32[]{:S(2)}) collective-permute-start(f32[128,128]{1,0:T(8,128)S(1)} %add.31.refs_4_), channel_id=1, source_target_pairs={{0,4},{4,0},{8,12},{12,8},{16,20},{20,16},{24,28},{28,24},{1,5},{5... | collective-permute-start | bytes 196616 | tf_op jit(solution)/shard_map/ppermute | solution.py:201
  35.9 1.5 %collective-permute-start.6 = (f32[64,128]{1,0:T(8,128)S(1)}, f32[64,128]{1,0:T(8,128)S(1)}, u32[]{:S(2)}, u32[]{:S(2)}) collective-permute-start(f32[64,128]{1,0:T(8,128)S(1)} %add.27.refs_0_), channel_id=1, source_target_pairs={{0,2},{1,3},{2,0},{3,1},{4,6},{5,7},{6,4},{7,5},{8,10},{9,11},{10,... | collective-permute-start | bytes 98312 | tf_op jit(solution)/shard_map/ppermute | solution.py:201
  37.4 2.5 %collective-permute-done.6.refs_2_ = f32[64,128]{1,0:T(8,128)S(1)} collective-permute-done((f32[64,128]{1,0:T(8,128)S(1)}, f32[64,128]{1,0:T(8,128)S(1)}, u32[]{:S(2)}, u32[]{:S(2)}) %collective-permute-start.6) | collective-permute-done | bytes 32800 | tf_op jit(solution)/shard_map/ppermute | solution.py:201
  40.0 3.9 %factor.1 = (f32[128,128]{1,0:T(8,128)}, bf16[256,256]{1,0:T(8,128)(2,1)S(1)}) custom-call(f32[64,128]{1,0:T(8,128)S(1)} %add.27.refs_0_, f32[64,128]{1,0:T(8,128)S(1)} %collective-permute-done.5.refs_1_, f32[64,128]{1,0:T(8,128)S(1)} %collective-permute-done.6.refs_2_, f32[64,128]{1,0:T(8,128)S(1)} %collective-permute-done.7.refs_3_), custom_call_target="tpu_custom_call" | custom-call | tf_op jit(solution)/shard_map/factor/pallas_call | solution.py:270
  43.9 2.8 %final.1 = (f32[128,512]{1,0:T(8,128)}, f32[2048,512]{1,0:T(8,128)}) custom-call(bf16[256,256]{1,0:T(8,128)(2,1)S(1)} %get-tuple-element.21.solve_ref, f32[2048,512]{1,0:T(8,128)S(1)} %copy-done, bf16[512,256]{1,0:T(8,128)(2,1)S(1)} %get-tuple-element.22.own_ref.refs_0_, bf16[512,256]{1,0:T(8,128)(2,1)S(1)} %get-tuple-element.23.mate_ref.refs_1_, ...), custom_call_target="tpu_custom_call" | custom-call | tf_op jit(solution)/shard_map/final/pallas_call | solution.py:282
  (15 shorter events, 0.1 us)
Async XLA Ops:
  0.6 9.5 %collective-permute-start.8 = (f32[512,128]{1,0:T(8,128)}, f32[512,128]{1,0:T(8,128)S(1)}, u32[]{:S(2)}, u32[]{:S(2)}) collective-permute-start(f32[512,128]{1,0:T(8,128)} %panel_ref.1), channel_id=1, source_target_pairs={{0,2},{1,3},{2,0},{3,1},{4,6},{5,7},{6,4},{7,5},{8,10},{9,11},{10,... | collective-permute-start | bytes 786440 | tf_op jit(solution)/shard_map/ppermute | solution.py:201
  3.7 7.9 %collective-permute-start = (f32[512,128]{1,0:T(8,128)}, f32[512,128]{1,0:T(8,128)S(1)}, u32[]{:S(2)}, u32[]{:S(2)}) collective-permute-start(f32[512,128]{1,0:T(8,128)} %panel_ref.1), channel_id=1, source_target_pairs={{0,1},{1,0},{2,3},{3,2},{4,5},{5,4},{6,7},{7,6},{8,9},{9,8},{10,11... | collective-permute-start | bytes 786440 | tf_op jit(solution)/shard_map/ppermute | solution.py:201
  10.2 4.7 %collective-permute-start.9 = (f32[512,128]{1,0:T(8,128)S(1)}, f32[512,128]{1,0:T(8,128)S(1)}, u32[]{:S(2)}, u32[]{:S(2)}) collective-permute-start(f32[512,128]{1,0:T(8,128)S(1)} %collective-permute-done.8.piece_ref), channel_id=1, source_target_pairs={{0,1},{1,0},{2,3},{3,2},{4,5},{5,4},{6,7},{7,6},{8,9},{9,8},{10,11... | collective-permute-start | bytes 786440 | tf_op jit(solution)/shard_map/ppermute | solution.py:201
  11.6 2.2 %copy-start = (f32[2048,512]{1,0:T(8,128)S(1)}, f32[2048,512]{1,0:T(8,128)}, u32[]{:S(2)}) copy-start(f32[2048,512]{1,0:T(8,128)} %held_ref.7) | copy-start | bytes 12582916
  15.4 6.8 %collective-permute-start.10 = (f32[128,128]{1,0:T(8,128)S(1)}, f32[128,128]{1,0:T(8,128)S(1)}, u32[]{:S(2)}, u32[]{:S(2)}) collective-permute-start(f32[128,128]{1,0:T(8,128)S(1)} %get-tuple-element.28), channel_id=1, source_target_pairs={{0,4},{4,0},{8,12},{12,8},{16,20},{20,16},{24,28},{28,24},{1,5},{5... | collective-permute-start | bytes 196616 | tf_op jit(solution)/shard_map/ppermute | solution.py:201
  17.2 5.2 %collective-permute-start.11 = (f32[128,128]{1,0:T(8,128)S(1)}, f32[128,128]{1,0:T(8,128)S(1)}, u32[]{:S(2)}, u32[]{:S(2)}) collective-permute-start(f32[128,128]{1,0:T(8,128)S(1)} %get-tuple-element.29), channel_id=1, source_target_pairs={{0,8},{4,12},{8,0},{12,4},{16,24},{20,28},{24,16},{28,20},{1,9},{5... | collective-permute-start | bytes 196616 | tf_op jit(solution)/shard_map/ppermute | solution.py:201
  18.8 5.5 %collective-permute-start.12 = (f32[128,128]{1,0:T(8,128)S(1)}, f32[128,128]{1,0:T(8,128)S(1)}, u32[]{:S(2)}, u32[]{:S(2)}) collective-permute-start(f32[128,128]{1,0:T(8,128)S(1)} %get-tuple-element.30), channel_id=1, source_target_pairs={{0,12},{4,8},{8,4},{12,0},{16,28},{20,24},{24,20},{28,16},{1,13},{... | collective-permute-start | bytes 196616 | tf_op jit(solution)/shard_map/ppermute | solution.py:201
  19.0 8.1 %collective-permute-start.3 = (f32[64,128]{1,0:T(8,128)S(1)}, f32[64,128]{1,0:T(8,128)S(1)}, u32[]{:S(2)}, u32[]{:S(2)}) collective-permute-start(f32[64,128]{1,0:T(8,128)S(1)} %get-tuple-element.19), channel_id=1, source_target_pairs={{0,12},{4,8},{8,4},{12,0},{16,28},{20,24},{24,20},{28,16},{1,13},{... | collective-permute-start | bytes 98312 | tf_op jit(solution)/shard_map/ppermute | solution.py:201
  21.8 5.3 %collective-permute-start.2 = (f32[64,128]{1,0:T(8,128)S(1)}, f32[64,128]{1,0:T(8,128)S(1)}, u32[]{:S(2)}, u32[]{:S(2)}) collective-permute-start(f32[64,128]{1,0:T(8,128)S(1)} %get-tuple-element.19), channel_id=1, source_target_pairs={{0,8},{4,12},{8,0},{12,4},{16,24},{20,28},{24,16},{28,20},{1,9},{5... | collective-permute-start | bytes 98312 | tf_op jit(solution)/shard_map/ppermute | solution.py:201
  22.2 4.9 %collective-permute-start.1 = (f32[64,128]{1,0:T(8,128)S(1)}, f32[64,128]{1,0:T(8,128)S(1)}, u32[]{:S(2)}, u32[]{:S(2)}) collective-permute-start(f32[64,128]{1,0:T(8,128)S(1)} %get-tuple-element.19), channel_id=1, source_target_pairs={{0,4},{4,0},{8,12},{12,8},{16,20},{20,16},{24,28},{28,24},{1,5},{5... | collective-permute-start | bytes 98312 | tf_op jit(solution)/shard_map/ppermute | solution.py:201
  24.4 7.9 %collective-permute-start.13 = (f32[128,128]{1,0:T(8,128)S(1)}, f32[128,128]{1,0:T(8,128)S(1)}, u32[]{:S(2)}, u32[]{:S(2)}) collective-permute-start(f32[128,128]{1,0:T(8,128)S(1)} %add_add_fusion), channel_id=1, source_target_pairs={{0,16},{4,20},{8,24},{12,28},{16,0},{20,4},{24,8},{28,12},{1,17},{... | collective-permute-start | bytes 196616 | tf_op jit(solution)/shard_map/ppermute | solution.py:201
  27.1 5.2 %collective-permute-start.4 = (f32[64,128]{1,0:T(8,128)S(1)}, f32[64,128]{1,0:T(8,128)S(1)}, u32[]{:S(2)}, u32[]{:S(2)}) collective-permute-start(f32[64,128]{1,0:T(8,128)S(1)} %add_add_fusion.1), channel_id=1, source_target_pairs={{0,16},{4,20},{8,24},{12,28},{16,0},{20,4},{24,8},{28,12},{1,17},{... | collective-permute-start | bytes 98312 | tf_op jit(solution)/shard_map/ppermute | solution.py:201
  32.3 5.1 %collective-permute-start.7 = (f32[64,128]{1,0:T(8,128)S(1)}, f32[64,128]{1,0:T(8,128)S(1)}, u32[]{:S(2)}, u32[]{:S(2)}) collective-permute-start(f32[64,128]{1,0:T(8,128)S(1)} %add.27.refs_0_), channel_id=1, source_target_pairs={{0,3},{1,2},{2,1},{3,0},{4,7},{5,6},{6,5},{7,4},{8,11},{9,10},{10,... | collective-permute-start | bytes 98312 | tf_op jit(solution)/shard_map/ppermute | solution.py:201
  32.3 11.5 %collective-permute-start.16 = (f32[128,128]{1,0:T(8,128)S(1)}, f32[128,128]{1,0:T(8,128)S(1)}, u32[]{:S(2)}, u32[]{:S(2)}) collective-permute-start(f32[128,128]{1,0:T(8,128)S(1)} %add.31.refs_4_), channel_id=1, source_target_pairs={{0,12},{4,8},{8,4},{12,0},{16,28},{20,24},{24,20},{28,16},{1,13},{... | collective-permute-start | bytes 196616 | tf_op jit(solution)/shard_map/ppermute | solution.py:201
  33.5 10.4 %collective-permute-start.15 = (f32[128,128]{1,0:T(8,128)S(1)}, f32[128,128]{1,0:T(8,128)S(1)}, u32[]{:S(2)}, u32[]{:S(2)}) collective-permute-start(f32[128,128]{1,0:T(8,128)S(1)} %add.31.refs_4_), channel_id=1, source_target_pairs={{0,8},{4,12},{8,0},{12,4},{16,24},{20,28},{24,16},{28,20},{1,9},{5... | collective-permute-start | bytes 196616 | tf_op jit(solution)/shard_map/ppermute | solution.py:201
  34.0 9.8 %collective-permute-start.14 = (f32[128,128]{1,0:T(8,128)S(1)}, f32[128,128]{1,0:T(8,128)S(1)}, u32[]{:S(2)}, u32[]{:S(2)}) collective-permute-start(f32[128,128]{1,0:T(8,128)S(1)} %add.31.refs_4_), channel_id=1, source_target_pairs={{0,4},{4,0},{8,12},{12,8},{16,20},{20,16},{24,28},{28,24},{1,5},{5... | collective-permute-start | bytes 196616 | tf_op jit(solution)/shard_map/ppermute | solution.py:201
  35.9 4.0 %collective-permute-start.6 = (f32[64,128]{1,0:T(8,128)S(1)}, f32[64,128]{1,0:T(8,128)S(1)}, u32[]{:S(2)}, u32[]{:S(2)}) collective-permute-start(f32[64,128]{1,0:T(8,128)S(1)} %add.27.refs_0_), channel_id=1, source_target_pairs={{0,2},{1,3},{2,0},{3,1},{4,6},{5,7},{6,4},{7,5},{8,10},{9,11},{10,... | collective-permute-start | bytes 98312 | tf_op jit(solution)/shard_map/ppermute | solution.py:201
  37.4 2.5 %collective-permute-start.5 = (f32[64,128]{1,0:T(8,128)S(1)}, f32[64,128]{1,0:T(8,128)S(1)}, u32[]{:S(2)}, u32[]{:S(2)}) collective-permute-start(f32[64,128]{1,0:T(8,128)S(1)} %add.27.refs_0_), channel_id=1, source_target_pairs={{0,1},{1,0},{2,3},{3,2},{4,5},{5,4},{6,7},{7,6},{8,9},{9,8},{10,11... | collective-permute-start | bytes 98312 | tf_op jit(solution)/shard_map/ppermute | solution.py:201

commit v4 on v3

--- a/solution.py
+++ b/solution.py
@@ -55,8 +55,8 @@
     return (lax.axis_index("col") ^ offset) * rows
 
 
-def part_of(offset, group):
-    return (lax.axis_index("row") & (group - 1)) ^ offset
+def part_of(slot, group):
+    return (lax.axis_index("row") & (group - 1)) ^ slot
 
 
 def wait_all(copies):
@@ -263,7 +263,10 @@
     )(pieces[-1], held, cross)
     splits.append(split_out)
 
-    gram = gram + sum(swap(gram, "row", k) for k in range(1, group))
+    found = [gram]
+    for k in range(1, group):
+        found.append(swap(gram, "row", k))
+    gram = sum(found[1:], found[0])
     for bit in row_bits[len(group_bits) :]:
         gram = gram + swap(gram, "row", bit)
     halves = [gram if o == 0 else swap(gram, "col", o) for f in offsets for o in (f, f ^ near)]
@@ -272,13 +275,14 @@
         out_shape=(square, jax.ShapeDtypeStruct((2 * width, 2 * width), jnp.bfloat16)),
         in_specs=[VMEM] * len(halves), out_specs=(VMEM, VMEM), compiler_params=limit(4), name="factor",
     )(*halves)
-    mine = parts[0]
     for k in range(1, group):
-        mine = mine + swap(parts[k], "row", k)
+        parts[k] = swap(parts[k], "row", k)
+    mine = sum(parts[1:], parts[0])
     for bit in row_bits[len(group_bits) :]:
         mine = mine + swap(mine, "row", bit)
-    others = [swap(mine, "row", k) for k in range(1, group)]
-
+    others = []
+    for k in range(1, group):
+        others.append(swap(mine, "row", k))
     w_scaled, remainder = pl.pallas_call(
         functools.partial(final_kernel, order=order, group=group, norm_scale=norm_scale, chunk=CHUNK),
         out_shape=(wide, f32(trailing_rows, columns)),

time: 46.9 us -> 46.9 us (level)
  no operation moved by 1% of the time
where the time goes in v4:
time: 46.9 us; the launch traced here: 46.7 us
  starting transfers between devices  19.5 us (42%)
  waiting for transfers between devices  14.5 us (31%)
  Pallas kernels  10.1 us (22%)
  local copies, waits for them, and re-layouts  1.74 us (4%)
  between operations  0.74 us (2%)
    ppermute x17, starting transfers between devices, swap(): return lax.ppermute(value, axis, [(i, i ^ bit) for i in range(size)])  19.5 us
    ppermute x17, waiting for transfers between devices, swap(): return lax.ppermute(value, axis, [(i, i ^ bit) for i in range(size)])  14.5 us
    pallas_call x1, Pallas kernels, body(): pl.pallas_call(functools.partial(factor_kernel, near=near, block=BLOCK, s...  3.93 us
    pallas_call x1, Pallas kernels, body(): pl.pallas_call(functools.partial(final_kernel, order=order, group=group,...  2.8 us
    unnamed x2, local copies, waits for them, and re-layouts  1.74 us
    pallas_call x1, Pallas kernels, body(): pl.pallas_call(own_kernel, out_shape=(square, split_shape), in_specs=[VME...  1.37 us
  transfers between devices with their start and end apart: 17, of which 4 were waited for; matrix products, arithmetic and copies ran while one was open for 0% of the time, Pallas kernels for 15%

profile of v4, /device:TPU:0, one launch (start us, length us, event | category | flops | bytes accessed | tf_op | source)
XLA Modules:
  0.0 46.7 jit_solution(6338166965565128293)
XLA Ops:
  0.6 3.0 %collective-permute-start.8 = (f32[512,128]{1,0:T(8,128)}, f32[512,128]{1,0:T(8,128)S(1)}, u32[]{:S(2)}, u32[]{:S(2)}) collective-permute-start(f32[512,128]{1,0:T(8,128)} %panel_ref.1), channel_id=1, source_target_pairs={{0,2},{1,3},{2,0},{3,1},{4,6},{5,7},{6,4},{7,5},{8,10},{9,11},{10,... | collective-permute-start | bytes 786440 | tf_op jit(solution)/shard_map/ppermute | solution.py:201
  3.7 0.0 collective-permute-start
  3.7 6.5 %collective-permute-done.8.piece_ref = f32[512,128]{1,0:T(8,128)S(1)} collective-permute-done((f32[512,128]{1,0:T(8,128)}, f32[512,128]{1,0:T(8,128)S(1)}, u32[]{:S(2)}, u32[]{:S(2)}) %collective-permute-start.8) | collective-permute-done | bytes 262176 | tf_op jit(solution)/shard_map/ppermute | solution.py:201
  10.2 1.4 %own.1 = (f32[128,128]{1,0:T(8,128)S(1)}, bf16[512,256]{1,0:T(8,128)(2,1)S(1)}) custom-call(f32[512,128]{1,0:T(8,128)} %panel_ref.1), custom_call_target="tpu_custom_call" | custom-call | flops 2147483648 | bytes 8388608 | tf_op jit(solution)/shard_map/own/pallas_call | solution.py:233
  11.6 0.0 copy-start
  11.6 0.4 mate.1
  12.0 1.7 %copy-done = f32[2048,512]{1,0:T(8,128)S(1)} copy-done((f32[2048,512]{1,0:T(8,128)S(1)}, f32[2048,512]{1,0:T(8,128)}, u32[]{:S(2)}) %copy-start) | copy-done | bytes 4194328
  13.7 0.6 %near.1.cross_in_ref = f32[128,512]{1,0:T(8,128)S(1)} custom-call(bf16[512,256]{1,0:T(8,128)(2,1)S(1)} %get-tuple-element.22.own_ref.refs_0_, bf16[512,256]{1,0:T(8,128)(2,1)S(1)} %get-tuple-element.23.mate_ref.refs_1_, f32[2048,512]{1,0:T(8,128)S(1)} %copy-done), custom_call_target="tpu_custom_call" | custom-call | tf_op jit(solution)/shard_map/near/pallas_call | solution.py:244
  14.4 0.5 far.1
  14.9 0.0 collective-permute-done.9.piece_ref
  14.9 0.5 %last.1 = (bf16[512,256]{1,0:T(8,128)(2,1)S(1)}, f32[128,128]{1,0:T(8,128)S(1)}, f32[128,128]{1,0:T(8,128)S(1)}, f32[128,128]{1,0:T(8,128)S(1)}, f32[128,128]{1,0:T(8,128)S(1)}) custom-call(f32[512,128]{1,0:T(8,128)S(1)} %collective-permute-done.9.piece_ref, f32[2048,512]{1,0:T(8,128)S(1)} %copy-done, f32[128,512]{1,0:T(8,128)S(1)} %get-tuple-element.25.cross_in_ref), custom_call_target="tpu_custom_call" | custom-call | tf_op jit(solution)/shard_map/last/pallas_call | solution.py:257
  15.4 1.8 %collective-permute-start.10 = (f32[128,128]{1,0:T(8,128)S(1)}, f32[128,128]{1,0:T(8,128)S(1)}, u32[]{:S(2)}, u32[]{:S(2)}) collective-permute-start(f32[128,128]{1,0:T(8,128)S(1)} %get-tuple-element.28), channel_id=1, source_target_pairs={{0,4},{4,0},{8,12},{12,8},{16,20},{20,16},{24,28},{28,24},{1,5},{5... | collective-permute-start | bytes 196616 | tf_op jit(solution)/shard_map/ppermute | solution.py:201
  17.2 1.6 %collective-permute-start.11 = (f32[128,128]{1,0:T(8,128)S(1)}, f32[128,128]{1,0:T(8,128)S(1)}, u32[]{:S(2)}, u32[]{:S(2)}) collective-permute-start(f32[128,128]{1,0:T(8,128)S(1)} %get-tuple-element.29), channel_id=1, source_target_pairs={{0,8},{4,12},{8,0},{12,4},{16,24},{20,28},{24,16},{28,20},{1,9},{5... | collective-permute-start | bytes 196616 | tf_op jit(solution)/shard_map/ppermute | solution.py:201
  18.8 0.1 collective-permute-start.12
  19.0 2.8 %collective-permute-start.3 = (f32[64,128]{1,0:T(8,128)S(1)}, f32[64,128]{1,0:T(8,128)S(1)}, u32[]{:S(2)}, u32[]{:S(2)}) collective-permute-start(f32[64,128]{1,0:T(8,128)S(1)} %get-tuple-element.19), channel_id=1, source_target_pairs={{0,12},{4,8},{8,4},{12,0},{16,28},{20,24},{24,20},{28,16},{1,13},{... | collective-permute-start | bytes 98312 | tf_op jit(solution)/shard_map/ppermute | solution.py:201
  21.8 0.4 collective-permute-start.2
  22.2 0.0 collective-permute-done.10
  22.2 0.3 collective-permute-start.1
  22.5 1.9 %collective-permute-done.12 = f32[128,128]{1,0:T(8,128)S(1)} collective-permute-done((f32[128,128]{1,0:T(8,128)S(1)}, f32[128,128]{1,0:T(8,128)S(1)}, u32[]{:S(2)}, u32[]{:S(2)}) %collective-permute-start.12) | collective-permute-done | bytes 65568 | tf_op jit(solution)/shard_map/ppermute | solution.py:201
  24.4 2.6 %collective-permute-start.13 = (f32[128,128]{1,0:T(8,128)S(1)}, f32[128,128]{1,0:T(8,128)S(1)}, u32[]{:S(2)}, u32[]{:S(2)}) collective-permute-start(f32[128,128]{1,0:T(8,128)S(1)} %add_add_fusion), channel_id=1, source_target_pairs={{0,16},{4,20},{8,24},{12,28},{16,0},{20,4},{24,8},{28,12},{1,17},{... | collective-permute-start | bytes 196616 | tf_op jit(solution)/shard_map/ppermute | solution.py:201
  27.0 0.0 collective-permute-done.3
  27.0 0.0 collective-permute-done.2
  27.1 1.7 %collective-permute-start.4 = (f32[64,128]{1,0:T(8,128)S(1)}, f32[64,128]{1,0:T(8,128)S(1)}, u32[]{:S(2)}, u32[]{:S(2)}) collective-permute-start(f32[64,128]{1,0:T(8,128)S(1)} %add_add_fusion.1), channel_id=1, source_target_pairs={{0,16},{4,20},{8,24},{12,28},{16,0},{20,4},{24,8},{28,12},{1,17},{... | collective-permute-start | bytes 98312 | tf_op jit(solution)/shard_map/ppermute | solution.py:201
  28.8 3.5 %collective-permute-done.4 = f32[64,128]{1,0:T(8,128)S(1)} collective-permute-done((f32[64,128]{1,0:T(8,128)S(1)}, f32[64,128]{1,0:T(8,128)S(1)}, u32[]{:S(2)}, u32[]{:S(2)}) %collective-permute-start.4) | collective-permute-done | bytes 32800 | tf_op jit(solution)/shard_map/ppermute | solution.py:201
  32.3 0.0 collective-permute-done.13
  32.3 1.1 %collective-permute-start.16 = (f32[128,128]{1,0:T(8,128)S(1)}, f32[128,128]{1,0:T(8,128)S(1)}, u32[]{:S(2)}, u32[]{:S(2)}) collective-permute-start(f32[128,128]{1,0:T(8,128)S(1)} %add.31.refs_4_), channel_id=1, source_target_pairs={{0,12},{4,8},{8,4},{12,0},{16,28},{20,24},{24,20},{28,16},{1,13},{... | collective-permute-start | bytes 196616 | tf_op jit(solution)/shard_map/ppermute | solution.py:201
  33.5 0.6 %collective-permute-start.15 = (f32[128,128]{1,0:T(8,128)S(1)}, f32[128,128]{1,0:T(8,128)S(1)}, u32[]{:S(2)}, u32[]{:S(2)}) collective-permute-start(f32[128,128]{1,0:T(8,128)S(1)} %add.31.refs_4_), channel_id=1, source_target_pairs={{0,8},{4,12},{8,0},{12,4},{16,24},{20,28},{24,16},{28,20},{1,9},{5... | collective-permute-start | bytes 196616 | tf_op jit(solution)/shard_map/ppermute | solution.py:201
  34.0 1.9 %collective-permute-start.14 = (f32[128,128]{1,0:T(8,128)S(1)}, f32[128,128]{1,0:T(8,128)S(1)}, u32[]{:S(2)}, u32[]{:S(2)}) collective-permute-start(f32[128,128]{1,0:T(8,128)S(1)} %add.31.refs_4_), channel_id=1, source_target_pairs={{0,4},{4,0},{8,12},{12,8},{16,20},{20,16},{24,28},{28,24},{1,5},{5... | collective-permute-start | bytes 196616 | tf_op jit(solution)/shard_map/ppermute | solution.py:201
  35.9 1.5 %collective-permute-start.6 = (f32[64,128]{1,0:T(8,128)S(1)}, f32[64,128]{1,0:T(8,128)S(1)}, u32[]{:S(2)}, u32[]{:S(2)}) collective-permute-start(f32[64,128]{1,0:T(8,128)S(1)} %add.27.refs_0_), channel_id=1, source_target_pairs={{0,2},{1,3},{2,0},{3,1},{4,6},{5,7},{6,4},{7,5},{8,10},{9,11},{10,... | collective-permute-start | bytes 98312 | tf_op jit(solution)/shard_map/ppermute | solution.py:201
  37.4 2.5 %collective-permute-done.6.refs_2_ = f32[64,128]{1,0:T(8,128)S(1)} collective-permute-done((f32[64,128]{1,0:T(8,128)S(1)}, f32[64,128]{1,0:T(8,128)S(1)}, u32[]{:S(2)}, u32[]{:S(2)}) %collective-permute-start.6) | collective-permute-done | bytes 32800 | tf_op jit(solution)/shard_map/ppermute | solution.py:201
  40.0 3.9 %factor.1 = (f32[128,128]{1,0:T(8,128)}, bf16[256,256]{1,0:T(8,128)(2,1)S(1)}) custom-call(f32[64,128]{1,0:T(8,128)S(1)} %add.27.refs_0_, f32[64,128]{1,0:T(8,128)S(1)} %collective-permute-done.5.refs_1_, f32[64,128]{1,0:T(8,128)S(1)} %collective-permute-done.6.refs_2_, f32[64,128]{1,0:T(8,128)S(1)} %collective-permute-done.7.refs_3_), custom_call_target="tpu_custom_call" | custom-call | tf_op jit(solution)/shard_map/factor/pallas_call | solution.py:273
  43.9 2.8 %final.1 = (f32[128,512]{1,0:T(8,128)}, f32[2048,512]{1,0:T(8,128)}) custom-call(bf16[256,256]{1,0:T(8,128)(2,1)S(1)} %get-tuple-element.21.solve_ref, f32[2048,512]{1,0:T(8,128)S(1)} %copy-done, bf16[512,256]{1,0:T(8,128)(2,1)S(1)} %get-tuple-element.22.own_ref.refs_0_, bf16[512,256]{1,0:T(8,128)(2,1)S(1)} %get-tuple-element.23.mate_ref.refs_1_, ...), custom_call_target="tpu_custom_call" | custom-call | tf_op jit(solution)/shard_map/final/pallas_call | solution.py:286
  (15 shorter events, 0.1 us)
Async XLA Ops:
  0.6 9.5 %collective-permute-start.8 = (f32[512,128]{1,0:T(8,128)}, f32[512,128]{1,0:T(8,128)S(1)}, u32[]{:S(2)}, u32[]{:S(2)}) collective-permute-start(f32[512,128]{1,0:T(8,128)} %panel_ref.1), channel_id=1, source_target_pairs={{0,2},{1,3},{2,0},{3,1},{4,6},{5,7},{6,4},{7,5},{8,10},{9,11},{10,... | collective-permute-start | bytes 786440 | tf_op jit(solution)/shard_map/ppermute | solution.py:201
  3.7 7.9 %collective-permute-start = (f32[512,128]{1,0:T(8,128)}, f32[512,128]{1,0:T(8,128)S(1)}, u32[]{:S(2)}, u32[]{:S(2)}) collective-permute-start(f32[512,128]{1,0:T(8,128)} %panel_ref.1), channel_id=1, source_target_pairs={{0,1},{1,0},{2,3},{3,2},{4,5},{5,4},{6,7},{7,6},{8,9},{9,8},{10,11... | collective-permute-start | bytes 786440 | tf_op jit(solution)/shard_map/ppermute | solution.py:201
  10.2 4.7 %collective-permute-start.9 = (f32[512,128]{1,0:T(8,128)S(1)}, f32[512,128]{1,0:T(8,128)S(1)}, u32[]{:S(2)}, u32[]{:S(2)}) collective-permute-start(f32[512,128]{1,0:T(8,128)S(1)} %collective-permute-done.8.piece_ref), channel_id=1, source_target_pairs={{0,1},{1,0},{2,3},{3,2},{4,5},{5,4},{6,7},{7,6},{8,9},{9,8},{10,11... | collective-permute-start | bytes 786440 | tf_op jit(solution)/shard_map/ppermute | solution.py:201
  11.6 2.2 %copy-start = (f32[2048,512]{1,0:T(8,128)S(1)}, f32[2048,512]{1,0:T(8,128)}, u32[]{:S(2)}) copy-start(f32[2048,512]{1,0:T(8,128)} %held_ref.7) | copy-start | bytes 12582916
  15.4 6.8 %collective-permute-start.10 = (f32[128,128]{1,0:T(8,128)S(1)}, f32[128,128]{1,0:T(8,128)S(1)}, u32[]{:S(2)}, u32[]{:S(2)}) collective-permute-start(f32[128,128]{1,0:T(8,128)S(1)} %get-tuple-element.28), channel_id=1, source_target_pairs={{0,4},{4,0},{8,12},{12,8},{16,20},{20,16},{24,28},{28,24},{1,5},{5... | collective-permute-start | bytes 196616 | tf_op jit(solution)/shard_map/ppermute | solution.py:201
  17.2 5.2 %collective-permute-start.11 = (f32[128,128]{1,0:T(8,128)S(1)}, f32[128,128]{1,0:T(8,128)S(1)}, u32[]{:S(2)}, u32[]{:S(2)}) collective-permute-start(f32[128,128]{1,0:T(8,128)S(1)} %get-tuple-element.29), channel_id=1, source_target_pairs={{0,8},{4,12},{8,0},{12,4},{16,24},{20,28},{24,16},{28,20},{1,9},{5... | collective-permute-start | bytes 196616 | tf_op jit(solution)/shard_map/ppermute | solution.py:201
  18.8 5.5 %collective-permute-start.12 = (f32[128,128]{1,0:T(8,128)S(1)}, f32[128,128]{1,0:T(8,128)S(1)}, u32[]{:S(2)}, u32[]{:S(2)}) collective-permute-start(f32[128,128]{1,0:T(8,128)S(1)} %get-tuple-element.30), channel_id=1, source_target_pairs={{0,12},{4,8},{8,4},{12,0},{16,28},{20,24},{24,20},{28,16},{1,13},{... | collective-permute-start | bytes 196616 | tf_op jit(solution)/shard_map/ppermute | solution.py:201
  19.0 8.1 %collective-permute-start.3 = (f32[64,128]{1,0:T(8,128)S(1)}, f32[64,128]{1,0:T(8,128)S(1)}, u32[]{:S(2)}, u32[]{:S(2)}) collective-permute-start(f32[64,128]{1,0:T(8,128)S(1)} %get-tuple-element.19), channel_id=1, source_target_pairs={{0,12},{4,8},{8,4},{12,0},{16,28},{20,24},{24,20},{28,16},{1,13},{... | collective-permute-start | bytes 98312 | tf_op jit(solution)/shard_map/ppermute | solution.py:201
  21.8 5.3 %collective-permute-start.2 = (f32[64,128]{1,0:T(8,128)S(1)}, f32[64,128]{1,0:T(8,128)S(1)}, u32[]{:S(2)}, u32[]{:S(2)}) collective-permute-start(f32[64,128]{1,0:T(8,128)S(1)} %get-tuple-element.19), channel_id=1, source_target_pairs={{0,8},{4,12},{8,0},{12,4},{16,24},{20,28},{24,16},{28,20},{1,9},{5... | collective-permute-start | bytes 98312 | tf_op jit(solution)/shard_map/ppermute | solution.py:201
  22.2 4.9 %collective-permute-start.1 = (f32[64,128]{1,0:T(8,128)S(1)}, f32[64,128]{1,0:T(8,128)S(1)}, u32[]{:S(2)}, u32[]{:S(2)}) collective-permute-start(f32[64,128]{1,0:T(8,128)S(1)} %get-tuple-element.19), channel_id=1, source_target_pairs={{0,4},{4,0},{8,12},{12,8},{16,20},{20,16},{24,28},{28,24},{1,5},{5... | collective-permute-start | bytes 98312 | tf_op jit(solution)/shard_map/ppermute | solution.py:201
  24.4 7.9 %collective-permute-start.13 = (f32[128,128]{1,0:T(8,128)S(1)}, f32[128,128]{1,0:T(8,128)S(1)}, u32[]{:S(2)}, u32[]{:S(2)}) collective-permute-start(f32[128,128]{1,0:T(8,128)S(1)} %add_add_fusion), channel_id=1, source_target_pairs={{0,16},{4,20},{8,24},{12,28},{16,0},{20,4},{24,8},{28,12},{1,17},{... | collective-permute-start | bytes 196616 | tf_op jit(solution)/shard_map/ppermute | solution.py:201
  27.1 5.2 %collective-permute-start.4 = (f32[64,128]{1,0:T(8,128)S(1)}, f32[64,128]{1,0:T(8,128)S(1)}, u32[]{:S(2)}, u32[]{:S(2)}) collective-permute-start(f32[64,128]{1,0:T(8,128)S(1)} %add_add_fusion.1), channel_id=1, source_target_pairs={{0,16},{4,20},{8,24},{12,28},{16,0},{20,4},{24,8},{28,12},{1,17},{... | collective-permute-start | bytes 98312 | tf_op jit(solution)/shard_map/ppermute | solution.py:201
  32.3 5.1 %collective-permute-start.7 = (f32[64,128]{1,0:T(8,128)S(1)}, f32[64,128]{1,0:T(8,128)S(1)}, u32[]{:S(2)}, u32[]{:S(2)}) collective-permute-start(f32[64,128]{1,0:T(8,128)S(1)} %add.27.refs_0_), channel_id=1, source_target_pairs={{0,3},{1,2},{2,1},{3,0},{4,7},{5,6},{6,5},{7,4},{8,11},{9,10},{10,... | collective-permute-start | bytes 98312 | tf_op jit(solution)/shard_map/ppermute | solution.py:201
  32.3 11.5 %collective-permute-start.16 = (f32[128,128]{1,0:T(8,128)S(1)}, f32[128,128]{1,0:T(8,128)S(1)}, u32[]{:S(2)}, u32[]{:S(2)}) collective-permute-start(f32[128,128]{1,0:T(8,128)S(1)} %add.31.refs_4_), channel_id=1, source_target_pairs={{0,12},{4,8},{8,4},{12,0},{16,28},{20,24},{24,20},{28,16},{1,13},{... | collective-permute-start | bytes 196616 | tf_op jit(solution)/shard_map/ppermute | solution.py:201
  33.5 10.4 %collective-permute-start.15 = (f32[128,128]{1,0:T(8,128)S(1)}, f32[128,128]{1,0:T(8,128)S(1)}, u32[]{:S(2)}, u32[]{:S(2)}) collective-permute-start(f32[128,128]{1,0:T(8,128)S(1)} %add.31.refs_4_), channel_id=1, source_target_pairs={{0,8},{4,12},{8,0},{12,4},{16,24},{20,28},{24,16},{28,20},{1,9},{5... | collective-permute-start | bytes 196616 | tf_op jit(solution)/shard_map/ppermute | solution.py:201
  34.0 9.8 %collective-permute-start.14 = (f32[128,128]{1,0:T(8,128)S(1)}, f32[128,128]{1,0:T(8,128)S(1)}, u32[]{:S(2)}, u32[]{:S(2)}) collective-permute-start(f32[128,128]{1,0:T(8,128)S(1)} %add.31.refs_4_), channel_id=1, source_target_pairs={{0,4},{4,0},{8,12},{12,8},{16,20},{20,16},{24,28},{28,24},{1,5},{5... | collective-permute-start | bytes 196616 | tf_op jit(solution)/shard_map/ppermute | solution.py:201
  35.9 4.0 %collective-permute-start.6 = (f32[64,128]{1,0:T(8,128)S(1)}, f32[64,128]{1,0:T(8,128)S(1)}, u32[]{:S(2)}, u32[]{:S(2)}) collective-permute-start(f32[64,128]{1,0:T(8,128)S(1)} %add.27.refs_0_), channel_id=1, source_target_pairs={{0,2},{1,3},{2,0},{3,1},{4,6},{5,7},{6,4},{7,5},{8,10},{9,11},{10,... | collective-permute-start | bytes 98312 | tf_op jit(solution)/shard_map/ppermute | solution.py:201
  37.4 2.5 %collective-permute-start.5 = (f32[64,128]{1,0:T(8,128)S(1)}, f32[64,128]{1,0:T(8,128)S(1)}, u32[]{:S(2)}, u32[]{:S(2)}) collective-permute-start(f32[64,128]{1,0:T(8,128)S(1)} %add.27.refs_0_), channel_id=1, source_target_pairs={{0,1},{1,0},{2,3},{3,2},{4,5},{5,4},{6,7},{7,6},{8,9},{9,8},{10,11... | collective-permute-start | bytes 98312 | tf_op jit(solution)/shard_map/ppermute | solution.py:201

commit v5 on v4

--- a/solution.py
+++ b/solution.py
@@ -142,9 +142,10 @@
                 head = jnp.where(local > k, ratio[:step], 0.0)
                 if ratio.shape[0] > step:
                     head = jnp.concatenate([head, ratio[step:]], 0)
-                ratio = head
-                left = left - ratio * left[k : k + 1, :]
-                right = right - ratio * right[k : k + 1, :]
+                columns[k] = head
+            for k in range(step):
+                left = left - columns[k] * left[k : k + 1, :]
+                right = right - columns[k] * right[k : k + 1, :]
             scale = lax.rsqrt(pivots)
             left_done.append(left[:step] * scale)
             right_done.append(right[:step] * scale)
@@ -153,8 +154,10 @@
         inverse_rows.append(jnp.where(lanes <= rows + first, jnp.concatenate(right_done, 0), 0.0))
         scaled_ref[first : first + block, :] = factor_rows[-1] * norm_scale
     inverse = jnp.concatenate(inverse_rows, 0)
-    solve = jnp.concatenate([inverse, dot(inverse, inverse, ((0,), (0,)), HIGHEST)], 0)
-    store_split(solve_ref, solve)
+    store_split(solve_ref.at[:width], inverse)
+    high, low = split(inverse)
+    left, right = jnp.concatenate([high, high, low], 0), jnp.concatenate([high, low, high], 0)
+    store_split(solve_ref.at[width:], dot(left, right, ((0,), (0,))))
 
 
 def final_kernel(solve_ref, held_ref, *refs, order, group, norm_scale, chunk):
@@ -162,19 +165,21 @@
     part_refs, (w_ref, remainder_ref, cross_ref, w_here, result, w_sem, sems) = refs[:group], refs[group:]
     width, part = part_refs[0].shape
     for k, part_ref in enumerate(part_refs):
-        cross_ref[:, pl.ds(pl.multiple_of(part_of(k, group) * part, part), part)] = part_ref[...]
+        where = pl.ds(pl.multiple_of(part_of(k, group) * part, part), part)
+        high, low = split(part_ref[...])
+        cross_ref[:width, where] = high
+        cross_ref[width : 2 * width, where] = high
+        cross_ref[2 * width :, where] = low
     contract = ((1,), (0,))
-    high, low = split(cross_ref[...])
-    both = solve_ref[...]
-    solved = dot(
-        jnp.concatenate([both, both[:, :width]], 1), jnp.concatenate([high, high, low], 0), contract
-    )
-    w_here[...] = solved[:width] * norm_scale
-    w_copy = pltpu.make_async_copy(w_here, w_ref, w_sem)
-    w_copy.start()
-    high, low = split(solved[width:])
+    before = cross_ref[...]
+
+    def solved(part):
+        both = solve_ref[part * width : (part + 1) * width, :]
+        return dot(jnp.concatenate([both, both[:, :width]], 1), before, contract)
+
+    high, low = split(solved(1))
     right = jnp.concatenate([high, high, low], 0)
-    copies = [w_copy]
+    copies = []
     rows = split_refs[0].shape[0]
     cuts = sems.shape[1]
     for i, split_ref in enumerate(split_refs):
@@ -193,6 +198,10 @@
                     pltpu.make_async_copy(result.at[i, here], remainder_ref.at[there], sems.at[i, n])
                 )
                 copies[-1].start()
+        if i == 0:
+            w_here[...] = solved(0) * norm_scale
+            copies.append(pltpu.make_async_copy(w_here, w_ref, w_sem))
+            copies[-1].start()
     wait_all(copies)
 
 
@@ -288,7 +297,7 @@
         out_shape=(wide, f32(trailing_rows, columns)),
         in_specs=[VMEM] * (2 + len(order) + group), out_specs=(HBM, HBM),
         scratch_shapes=[
-            pltpu.VMEM((width, columns), jnp.float32),
+            pltpu.VMEM((3 * width, columns), jnp.bfloat16),
             pltpu.VMEM((width, columns), jnp.float32),
             pltpu.VMEM((len(order), piece_rows, columns), jnp.float32),
             copies,

time: 46.9 us -> 46.8 us (level)
  no operation moved by 1% of the time
where the time goes in v5:
time: 46.8 us; the launch traced here: 46.6 us
  starting transfers between devices  19.5 us (42%)
  waiting for transfers between devices  14.5 us (31%)
  Pallas kernels  10 us (21%)
  local copies, waits for them, and re-layouts  1.74 us (4%)
  between operations  0.74 us (2%)
    ppermute x17, starting transfers between devices, swap(): return lax.ppermute(value, axis, [(i, i ^ bit) for i in range(size)])  19.5 us
    ppermute x17, waiting for transfers between devices, swap(): return lax.ppermute(value, axis, [(i, i ^ bit) for i in range(size)])  14.5 us
    pallas_call x1, Pallas kernels, body(): pl.pallas_call(functools.partial(factor_kernel, near=near, block=BLOCK, s...  3.88 us
    pallas_call x1, Pallas kernels, body(): pl.pallas_call(functools.partial(final_kernel, order=order, group=group,...  2.75 us
    unnamed x2, local copies, waits for them, and re-layouts  1.74 us
    pallas_call x1, Pallas kernels, body(): pl.pallas_call(own_kernel, out_shape=(square, split_shape), in_specs=[VME...  1.37 us
  transfers between devices with their start and end apart: 17, of which 4 were waited for; matrix products, arithmetic and copies ran while one was open for 0% of the time, Pallas kernels for 15%

profile of v5, /device:TPU:0, one launch (start us, length us, event | category | flops | bytes accessed | tf_op | source)
XLA Modules:
  0.0 46.6 jit_solution(18205499130485859423)
XLA Ops:
  0.6 3.0 %collective-permute-start.8 = (f32[512,128]{1,0:T(8,128)}, f32[512,128]{1,0:T(8,128)S(1)}, u32[]{:S(2)}, u32[]{:S(2)}) collective-permute-start(f32[512,128]{1,0:T(8,128)} %panel_ref.1), channel_id=1, source_target_pairs={{0,2},{1,3},{2,0},{3,1},{4,6},{5,7},{6,4},{7,5},{8,10},{9,11},{10,... | collective-permute-start | bytes 786440 | tf_op jit(solution)/shard_map/ppermute | solution.py:210
  3.7 0.0 collective-permute-start
  3.7 6.5 %collective-permute-done.8.piece_ref = f32[512,128]{1,0:T(8,128)S(1)} collective-permute-done((f32[512,128]{1,0:T(8,128)}, f32[512,128]{1,0:T(8,128)S(1)}, u32[]{:S(2)}, u32[]{:S(2)}) %collective-permute-start.8) | collective-permute-done | bytes 262176 | tf_op jit(solution)/shard_map/ppermute | solution.py:210
  10.2 1.4 %own.1 = (f32[128,128]{1,0:T(8,128)S(1)}, bf16[512,256]{1,0:T(8,128)(2,1)S(1)}) custom-call(f32[512,128]{1,0:T(8,128)} %panel_ref.1), custom_call_target="tpu_custom_call" | custom-call | flops 2147483648 | bytes 8388608 | tf_op jit(solution)/shard_map/own/pallas_call | solution.py:242
  11.6 0.0 copy-start
  11.6 0.4 mate.1
  12.0 1.7 %copy-done = f32[2048,512]{1,0:T(8,128)S(1)} copy-done((f32[2048,512]{1,0:T(8,128)S(1)}, f32[2048,512]{1,0:T(8,128)}, u32[]{:S(2)}) %copy-start) | copy-done | bytes 4194328
  13.7 0.6 %near.1.cross_in_ref = f32[128,512]{1,0:T(8,128)S(1)} custom-call(bf16[512,256]{1,0:T(8,128)(2,1)S(1)} %get-tuple-element.22.own_ref.refs_0_, bf16[512,256]{1,0:T(8,128)(2,1)S(1)} %get-tuple-element.23.mate_ref.refs_1_, f32[2048,512]{1,0:T(8,128)S(1)} %copy-done), custom_call_target="tpu_custom_call" | custom-call | tf_op jit(solution)/shard_map/near/pallas_call | solution.py:253
  14.4 0.5 far.1
  14.9 0.0 collective-permute-done.9.piece_ref
  14.9 0.5 %last.1 = (bf16[512,256]{1,0:T(8,128)(2,1)S(1)}, f32[128,128]{1,0:T(8,128)S(1)}, f32[128,128]{1,0:T(8,128)S(1)}, f32[128,128]{1,0:T(8,128)S(1)}, f32[128,128]{1,0:T(8,128)S(1)}) custom-call(f32[512,128]{1,0:T(8,128)S(1)} %collective-permute-done.9.piece_ref, f32[2048,512]{1,0:T(8,128)S(1)} %copy-done, f32[128,512]{1,0:T(8,128)S(1)} %get-tuple-element.25.cross_in_ref), custom_call_target="tpu_custom_call" | custom-call | tf_op jit(solution)/shard_map/last/pallas_call | solution.py:266
  15.4 1.8 %collective-permute-start.10 = (f32[128,128]{1,0:T(8,128)S(1)}, f32[128,128]{1,0:T(8,128)S(1)}, u32[]{:S(2)}, u32[]{:S(2)}) collective-permute-start(f32[128,128]{1,0:T(8,128)S(1)} %get-tuple-element.28), channel_id=1, source_target_pairs={{0,4},{4,0},{8,12},{12,8},{16,20},{20,16},{24,28},{28,24},{1,5},{5... | collective-permute-start | bytes 196616 | tf_op jit(solution)/shard_map/ppermute | solution.py:210
  17.2 1.6 %collective-permute-start.11 = (f32[128,128]{1,0:T(8,128)S(1)}, f32[128,128]{1,0:T(8,128)S(1)}, u32[]{:S(2)}, u32[]{:S(2)}) collective-permute-start(f32[128,128]{1,0:T(8,128)S(1)} %get-tuple-element.29), channel_id=1, source_target_pairs={{0,8},{4,12},{8,0},{12,4},{16,24},{20,28},{24,16},{28,20},{1,9},{5... | collective-permute-start | bytes 196616 | tf_op jit(solution)/shard_map/ppermute | solution.py:210
  18.8 0.1 collective-permute-start.12
  19.0 2.8 %collective-permute-start.3 = (f32[64,128]{1,0:T(8,128)S(1)}, f32[64,128]{1,0:T(8,128)S(1)}, u32[]{:S(2)}, u32[]{:S(2)}) collective-permute-start(f32[64,128]{1,0:T(8,128)S(1)} %get-tuple-element.19), channel_id=1, source_target_pairs={{0,12},{4,8},{8,4},{12,0},{16,28},{20,24},{24,20},{28,16},{1,13},{... | collective-permute-start | bytes 98312 | tf_op jit(solution)/shard_map/ppermute | solution.py:210
  21.8 0.4 collective-permute-start.2
  22.2 0.0 collective-permute-done.10
  22.2 0.3 collective-permute-start.1
  22.5 1.9 %collective-permute-done.12 = f32[128,128]{1,0:T(8,128)S(1)} collective-permute-done((f32[128,128]{1,0:T(8,128)S(1)}, f32[128,128]{1,0:T(8,128)S(1)}, u32[]{:S(2)}, u32[]{:S(2)}) %collective-permute-start.12) | collective-permute-done | bytes 65568 | tf_op jit(solution)/shard_map/ppermute | solution.py:210
  24.4 2.6 %collective-permute-start.13 = (f32[128,128]{1,0:T(8,128)S(1)}, f32[128,128]{1,0:T(8,128)S(1)}, u32[]{:S(2)}, u32[]{:S(2)}) collective-permute-start(f32[128,128]{1,0:T(8,128)S(1)} %add_add_fusion), channel_id=1, source_target_pairs={{0,16},{4,20},{8,24},{12,28},{16,0},{20,4},{24,8},{28,12},{1,17},{... | collective-permute-start | bytes 196616 | tf_op jit(solution)/shard_map/ppermute | solution.py:210
  27.0 0.0 collective-permute-done.3
  27.0 0.0 collective-permute-done.2
  27.1 1.7 %collective-permute-start.4 = (f32[64,128]{1,0:T(8,128)S(1)}, f32[64,128]{1,0:T(8,128)S(1)}, u32[]{:S(2)}, u32[]{:S(2)}) collective-permute-start(f32[64,128]{1,0:T(8,128)S(1)} %add_add_fusion.1), channel_id=1, source_target_pairs={{0,16},{4,20},{8,24},{12,28},{16,0},{20,4},{24,8},{28,12},{1,17},{... | collective-permute-start | bytes 98312 | tf_op jit(solution)/shard_map/ppermute | solution.py:210
  28.8 3.5 %collective-permute-done.4 = f32[64,128]{1,0:T(8,128)S(1)} collective-permute-done((f32[64,128]{1,0:T(8,128)S(1)}, f32[64,128]{1,0:T(8,128)S(1)}, u32[]{:S(2)}, u32[]{:S(2)}) %collective-permute-start.4) | collective-permute-done | bytes 32800 | tf_op jit(solution)/shard_map/ppermute | solution.py:210
  32.3 0.0 collective-permute-done.13
  32.3 1.1 %collective-permute-start.16 = (f32[128,128]{1,0:T(8,128)S(1)}, f32[128,128]{1,0:T(8,128)S(1)}, u32[]{:S(2)}, u32[]{:S(2)}) collective-permute-start(f32[128,128]{1,0:T(8,128)S(1)} %add.31.refs_4_), channel_id=1, source_target_pairs={{0,12},{4,8},{8,4},{12,0},{16,28},{20,24},{24,20},{28,16},{1,13},{... | collective-permute-start | bytes 196616 | tf_op jit(solution)/shard_map/ppermute | solution.py:210
  33.5 0.6 %collective-permute-start.15 = (f32[128,128]{1,0:T(8,128)S(1)}, f32[128,128]{1,0:T(8,128)S(1)}, u32[]{:S(2)}, u32[]{:S(2)}) collective-permute-start(f32[128,128]{1,0:T(8,128)S(1)} %add.31.refs_4_), channel_id=1, source_target_pairs={{0,8},{4,12},{8,0},{12,4},{16,24},{20,28},{24,16},{28,20},{1,9},{5... | collective-permute-start | bytes 196616 | tf_op jit(solution)/shard_map/ppermute | solution.py:210
  34.0 1.9 %collective-permute-start.14 = (f32[128,128]{1,0:T(8,128)S(1)}, f32[128,128]{1,0:T(8,128)S(1)}, u32[]{:S(2)}, u32[]{:S(2)}) collective-permute-start(f32[128,128]{1,0:T(8,128)S(1)} %add.31.refs_4_), channel_id=1, source_target_pairs={{0,4},{4,0},{8,12},{12,8},{16,20},{20,16},{24,28},{28,24},{1,5},{5... | collective-permute-start | bytes 196616 | tf_op jit(solution)/shard_map/ppermute | solution.py:210
  35.9 1.5 %collective-permute-start.6 = (f32[64,128]{1,0:T(8,128)S(1)}, f32[64,128]{1,0:T(8,128)S(1)}, u32[]{:S(2)}, u32[]{:S(2)}) collective-permute-start(f32[64,128]{1,0:T(8,128)S(1)} %add.27.refs_0_), channel_id=1, source_target_pairs={{0,2},{1,3},{2,0},{3,1},{4,6},{5,7},{6,4},{7,5},{8,10},{9,11},{10,... | collective-permute-start | bytes 98312 | tf_op jit(solution)/shard_map/ppermute | solution.py:210
  37.4 2.5 %collective-permute-done.6.refs_2_ = f32[64,128]{1,0:T(8,128)S(1)} collective-permute-done((f32[64,128]{1,0:T(8,128)S(1)}, f32[64,128]{1,0:T(8,128)S(1)}, u32[]{:S(2)}, u32[]{:S(2)}) %collective-permute-start.6) | collective-permute-done | bytes 32800 | tf_op jit(solution)/shard_map/ppermute | solution.py:210
  40.0 3.9 %factor.1 = (f32[128,128]{1,0:T(8,128)}, bf16[256,256]{1,0:T(8,128)(2,1)S(1)}) custom-call(f32[64,128]{1,0:T(8,128)S(1)} %add.27.refs_0_, f32[64,128]{1,0:T(8,128)S(1)} %collective-permute-done.5.refs_1_, f32[64,128]{1,0:T(8,128)S(1)} %collective-permute-done.6.refs_2_, f32[64,128]{1,0:T(8,128)S(1)} %collective-permute-done.7.refs_3_), custom_call_target="tpu_custom_call" | custom-call | tf_op jit(solution)/shard_map/factor/pallas_call | solution.py:282
  43.8 2.8 %final.1 = (f32[128,512]{1,0:T(8,128)}, f32[2048,512]{1,0:T(8,128)}) custom-call(bf16[256,256]{1,0:T(8,128)(2,1)S(1)} %get-tuple-element.21.solve_ref, f32[2048,512]{1,0:T(8,128)S(1)} %copy-done, bf16[512,256]{1,0:T(8,128)(2,1)S(1)} %get-tuple-element.22.own_ref.refs_0_, bf16[512,256]{1,0:T(8,128)(2,1)S(1)} %get-tuple-element.23.mate_ref.refs_1_, ...), custom_call_target="tpu_custom_call" | custom-call | tf_op jit(solution)/shard_map/final/pallas_call | solution.py:295
  (15 shorter events, 0.1 us)
Async XLA Ops:
  0.6 9.5 %collective-permute-start.8 = (f32[512,128]{1,0:T(8,128)}, f32[512,128]{1,0:T(8,128)S(1)}, u32[]{:S(2)}, u32[]{:S(2)}) collective-permute-start(f32[512,128]{1,0:T(8,128)} %panel_ref.1), channel_id=1, source_target_pairs={{0,2},{1,3},{2,0},{3,1},{4,6},{5,7},{6,4},{7,5},{8,10},{9,11},{10,... | collective-permute-start | bytes 786440 | tf_op jit(solution)/shard_map/ppermute | solution.py:210
  3.7 7.9 %collective-permute-start = (f32[512,128]{1,0:T(8,128)}, f32[512,128]{1,0:T(8,128)S(1)}, u32[]{:S(2)}, u32[]{:S(2)}) collective-permute-start(f32[512,128]{1,0:T(8,128)} %panel_ref.1), channel_id=1, source_target_pairs={{0,1},{1,0},{2,3},{3,2},{4,5},{5,4},{6,7},{7,6},{8,9},{9,8},{10,11... | collective-permute-start | bytes 786440 | tf_op jit(solution)/shard_map/ppermute | solution.py:210
  10.2 4.7 %collective-permute-start.9 = (f32[512,128]{1,0:T(8,128)S(1)}, f32[512,128]{1,0:T(8,128)S(1)}, u32[]{:S(2)}, u32[]{:S(2)}) collective-permute-start(f32[512,128]{1,0:T(8,128)S(1)} %collective-permute-done.8.piece_ref), channel_id=1, source_target_pairs={{0,1},{1,0},{2,3},{3,2},{4,5},{5,4},{6,7},{7,6},{8,9},{9,8},{10,11... | collective-permute-start | bytes 786440 | tf_op jit(solution)/shard_map/ppermute | solution.py:210
  11.6 2.2 %copy-start = (f32[2048,512]{1,0:T(8,128)S(1)}, f32[2048,512]{1,0:T(8,128)}, u32[]{:S(2)}) copy-start(f32[2048,512]{1,0:T(8,128)} %held_ref.7) | copy-start | bytes 12582916
  15.4 6.8 %collective-permute-start.10 = (f32[128,128]{1,0:T(8,128)S(1)}, f32[128,128]{1,0:T(8,128)S(1)}, u32[]{:S(2)}, u32[]{:S(2)}) collective-permute-start(f32[128,128]{1,0:T(8,128)S(1)} %get-tuple-element.28), channel_id=1, source_target_pairs={{0,4},{4,0},{8,12},{12,8},{16,20},{20,16},{24,28},{28,24},{1,5},{5... | collective-permute-start | bytes 196616 | tf_op jit(solution)/shard_map/ppermute | solution.py:210
  17.2 5.2 %collective-permute-start.11 = (f32[128,128]{1,0:T(8,128)S(1)}, f32[128,128]{1,0:T(8,128)S(1)}, u32[]{:S(2)}, u32[]{:S(2)}) collective-permute-start(f32[128,128]{1,0:T(8,128)S(1)} %get-tuple-element.29), channel_id=1, source_target_pairs={{0,8},{4,12},{8,0},{12,4},{16,24},{20,28},{24,16},{28,20},{1,9},{5... | collective-permute-start | bytes 196616 | tf_op jit(solution)/shard_map/ppermute | solution.py:210
  18.8 5.5 %collective-permute-start.12 = (f32[128,128]{1,0:T(8,128)S(1)}, f32[128,128]{1,0:T(8,128)S(1)}, u32[]{:S(2)}, u32[]{:S(2)}) collective-permute-start(f32[128,128]{1,0:T(8,128)S(1)} %get-tuple-element.30), channel_id=1, source_target_pairs={{0,12},{4,8},{8,4},{12,0},{16,28},{20,24},{24,20},{28,16},{1,13},{... | collective-permute-start | bytes 196616 | tf_op jit(solution)/shard_map/ppermute | solution.py:210
  19.0 8.1 %collective-permute-start.3 = (f32[64,128]{1,0:T(8,128)S(1)}, f32[64,128]{1,0:T(8,128)S(1)}, u32[]{:S(2)}, u32[]{:S(2)}) collective-permute-start(f32[64,128]{1,0:T(8,128)S(1)} %get-tuple-element.19), channel_id=1, source_target_pairs={{0,12},{4,8},{8,4},{12,0},{16,28},{20,24},{24,20},{28,16},{1,13},{... | collective-permute-start | bytes 98312 | tf_op jit(solution)/shard_map/ppermute | solution.py:210
  21.8 5.3 %collective-permute-start.2 = (f32[64,128]{1,0:T(8,128)S(1)}, f32[64,128]{1,0:T(8,128)S(1)}, u32[]{:S(2)}, u32[]{:S(2)}) collective-permute-start(f32[64,128]{1,0:T(8,128)S(1)} %get-tuple-element.19), channel_id=1, source_target_pairs={{0,8},{4,12},{8,0},{12,4},{16,24},{20,28},{24,16},{28,20},{1,9},{5... | collective-permute-start | bytes 98312 | tf_op jit(solution)/shard_map/ppermute | solution.py:210
  22.2 4.9 %collective-permute-start.1 = (f32[64,128]{1,0:T(8,128)S(1)}, f32[64,128]{1,0:T(8,128)S(1)}, u32[]{:S(2)}, u32[]{:S(2)}) collective-permute-start(f32[64,128]{1,0:T(8,128)S(1)} %get-tuple-element.19), channel_id=1, source_target_pairs={{0,4},{4,0},{8,12},{12,8},{16,20},{20,16},{24,28},{28,24},{1,5},{5... | collective-permute-start | bytes 98312 | tf_op jit(solution)/shard_map/ppermute | solution.py:210
  24.4 7.9 %collective-permute-start.13 = (f32[128,128]{1,0:T(8,128)S(1)}, f32[128,128]{1,0:T(8,128)S(1)}, u32[]{:S(2)}, u32[]{:S(2)}) collective-permute-start(f32[128,128]{1,0:T(8,128)S(1)} %add_add_fusion), channel_id=1, source_target_pairs={{0,16},{4,20},{8,24},{12,28},{16,0},{20,4},{24,8},{28,12},{1,17},{... | collective-permute-start | bytes 196616 | tf_op jit(solution)/shard_map/ppermute | solution.py:210
  27.1 5.2 %collective-permute-start.4 = (f32[64,128]{1,0:T(8,128)S(1)}, f32[64,128]{1,0:T(8,128)S(1)}, u32[]{:S(2)}, u32[]{:S(2)}) collective-permute-start(f32[64,128]{1,0:T(8,128)S(1)} %add_add_fusion.1), channel_id=1, source_target_pairs={{0,16},{4,20},{8,24},{12,28},{16,0},{20,4},{24,8},{28,12},{1,17},{... | collective-permute-start | bytes 98312 | tf_op jit(solution)/shard_map/ppermute | solution.py:210
  32.3 5.1 %collective-permute-start.7 = (f32[64,128]{1,0:T(8,128)S(1)}, f32[64,128]{1,0:T(8,128)S(1)}, u32[]{:S(2)}, u32[]{:S(2)}) collective-permute-start(f32[64,128]{1,0:T(8,128)S(1)} %add.27.refs_0_), channel_id=1, source_target_pairs={{0,3},{1,2},{2,1},{3,0},{4,7},{5,6},{6,5},{7,4},{8,11},{9,10},{10,... | collective-permute-start | bytes 98312 | tf_op jit(solution)/shard_map/ppermute | solution.py:210
  32.3 11.5 %collective-permute-start.16 = (f32[128,128]{1,0:T(8,128)S(1)}, f32[128,128]{1,0:T(8,128)S(1)}, u32[]{:S(2)}, u32[]{:S(2)}) collective-permute-start(f32[128,128]{1,0:T(8,128)S(1)} %add.31.refs_4_), channel_id=1, source_target_pairs={{0,12},{4,8},{8,4},{12,0},{16,28},{20,24},{24,20},{28,16},{1,13},{... | collective-permute-start | bytes 196616 | tf_op jit(solution)/shard_map/ppermute | solution.py:210
  33.5 10.4 %collective-permute-start.15 = (f32[128,128]{1,0:T(8,128)S(1)}, f32[128,128]{1,0:T(8,128)S(1)}, u32[]{:S(2)}, u32[]{:S(2)}) collective-permute-start(f32[128,128]{1,0:T(8,128)S(1)} %add.31.refs_4_), channel_id=1, source_target_pairs={{0,8},{4,12},{8,0},{12,4},{16,24},{20,28},{24,16},{28,20},{1,9},{5... | collective-permute-start | bytes 196616 | tf_op jit(solution)/shard_map/ppermute | solution.py:210
  34.0 9.8 %collective-permute-start.14 = (f32[128,128]{1,0:T(8,128)S(1)}, f32[128,128]{1,0:T(8,128)S(1)}, u32[]{:S(2)}, u32[]{:S(2)}) collective-permute-start(f32[128,128]{1,0:T(8,128)S(1)} %add.31.refs_4_), channel_id=1, source_target_pairs={{0,4},{4,0},{8,12},{12,8},{16,20},{20,16},{24,28},{28,24},{1,5},{5... | collective-permute-start | bytes 196616 | tf_op jit(solution)/shard_map/ppermute | solution.py:210
  35.9 4.0 %collective-permute-start.6 = (f32[64,128]{1,0:T(8,128)S(1)}, f32[64,128]{1,0:T(8,128)S(1)}, u32[]{:S(2)}, u32[]{:S(2)}) collective-permute-start(f32[64,128]{1,0:T(8,128)S(1)} %add.27.refs_0_), channel_id=1, source_target_pairs={{0,2},{1,3},{2,0},{3,1},{4,6},{5,7},{6,4},{7,5},{8,10},{9,11},{10,... | collective-permute-start | bytes 98312 | tf_op jit(solution)/shard_map/ppermute | solution.py:210
  37.4 2.5 %collective-permute-start.5 = (f32[64,128]{1,0:T(8,128)S(1)}, f32[64,128]{1,0:T(8,128)S(1)}, u32[]{:S(2)}, u32[]{:S(2)}) collective-permute-start(f32[64,128]{1,0:T(8,128)S(1)} %add.27.refs_0_), channel_id=1, source_target_pairs={{0,1},{1,0},{2,3},{3,2},{4,5},{5,4},{6,7},{7,6},{8,9},{9,8},{10,11... | collective-permute-start | bytes 98312 | tf_op jit(solution)/shard_map/ppermute | solution.py:210

commit v6 on v5

--- a/solution.py
+++ b/solution.py
@@ -10,7 +10,7 @@
 
 
 HIGHEST = lax.Precision.HIGHEST
-CUTS = 2
+CUTS = 4
 BLOCK, STEP = 32, 16
 COST = pl.CostEstimate(flops=1 << 31, bytes_accessed=1 << 23, transcendentals=0)
 CHUNK = 128
@@ -165,13 +165,10 @@
     part_refs, (w_ref, remainder_ref, cross_ref, w_here, result, w_sem, sems) = refs[:group], refs[group:]
     width, part = part_refs[0].shape
     for k, part_ref in enumerate(part_refs):
-        where = pl.ds(pl.multiple_of(part_of(k, group) * part, part), part)
-        high, low = split(part_ref[...])
-        cross_ref[:width, where] = high
-        cross_ref[width : 2 * width, where] = high
-        cross_ref[2 * width :, where] = low
+        cross_ref[:, pl.ds(pl.multiple_of(part_of(k, group) * part, part), part)] = part_ref[...]
     contract = ((1,), (0,))
-    before = cross_ref[...]
+    high, low = split(cross_ref[...])
+    before = jnp.concatenate([high, high, low], 0)
 
     def solved(part):
         both = solve_ref[part * width : (part + 1) * width, :]
@@ -297,7 +294,7 @@
         out_shape=(wide, f32(trailing_rows, columns)),
         in_specs=[VMEM] * (2 + len(order) + group), out_specs=(HBM, HBM),
         scratch_shapes=[
-            pltpu.VMEM((3 * width, columns), jnp.bfloat16),
+            pltpu.VMEM((width, columns), jnp.float32),
             pltpu.VMEM((width, columns), jnp.float32),
             pltpu.VMEM((len(order), piece_rows, columns), jnp.float32),
             copies,

time: 46.8 us -> 46.8 us (level)
  no operation moved by 1% of the time
where the time goes in v6:
time: 46.8 us; the launch traced here: 46.6 us
  starting transfers between devices  19.5 us (42%)
  waiting for transfers between devices  14.5 us (31%)
  Pallas kernels  10 us (21%)
  local copies, waits for them, and re-layouts  1.74 us (4%)
  between operations  0.74 us (2%)
    ppermute x17, starting transfers between devices, swap(): return lax.ppermute(value, axis, [(i, i ^ bit) for i in range(size)])  19.5 us
    ppermute x17, waiting for transfers between devices, swap(): return lax.ppermute(value, axis, [(i, i ^ bit) for i in range(size)])  14.5 us
    pallas_call x1, Pallas kernels, body(): pl.pallas_call(functools.partial(factor_kernel, near=near, block=BLOCK, s...  3.88 us
    pallas_call x1, Pallas kernels, body(): pl.pallas_call(functools.partial(final_kernel, order=order, group=group,...  2.72 us
    unnamed x2, local copies, waits for them, and re-layouts  1.74 us
    pallas_call x1, Pallas kernels, body(): pl.pallas_call(own_kernel, out_shape=(square, split_shape), in_specs=[VME...  1.37 us
  transfers between devices with their start and end apart: 17, of which 4 were waited for; matrix products, arithmetic and copies ran while one was open for 0% of the time, Pallas kernels for 15%

profile of v6, /device:TPU:0, one launch (start us, length us, event | category | flops | bytes accessed | tf_op | source)
XLA Modules:
  0.0 46.6 jit_solution(11163767866341989473)
XLA Ops:
  0.6 3.0 %collective-permute-start.8 = (f32[512,128]{1,0:T(8,128)}, f32[512,128]{1,0:T(8,128)S(1)}, u32[]{:S(2)}, u32[]{:S(2)}) collective-permute-start(f32[512,128]{1,0:T(8,128)} %panel_ref.1), channel_id=1, source_target_pairs={{0,2},{1,3},{2,0},{3,1},{4,6},{5,7},{6,4},{7,5},{8,10},{9,11},{10,... | collective-permute-start | bytes 786440 | tf_op jit(solution)/shard_map/ppermute | solution.py:207
  3.7 0.0 collective-permute-start
  3.7 6.5 %collective-permute-done.8.piece_ref = f32[512,128]{1,0:T(8,128)S(1)} collective-permute-done((f32[512,128]{1,0:T(8,128)}, f32[512,128]{1,0:T(8,128)S(1)}, u32[]{:S(2)}, u32[]{:S(2)}) %collective-permute-start.8) | collective-permute-done | bytes 262176 | tf_op jit(solution)/shard_map/ppermute | solution.py:207
  10.2 1.4 %own.1 = (f32[128,128]{1,0:T(8,128)S(1)}, bf16[512,256]{1,0:T(8,128)(2,1)S(1)}) custom-call(f32[512,128]{1,0:T(8,128)} %panel_ref.1), custom_call_target="tpu_custom_call" | custom-call | flops 2147483648 | bytes 8388608 | tf_op jit(solution)/shard_map/own/pallas_call | solution.py:239
  11.6 0.0 copy-start
  11.6 0.4 mate.1
  12.0 1.7 %copy-done = f32[2048,512]{1,0:T(8,128)S(1)} copy-done((f32[2048,512]{1,0:T(8,128)S(1)}, f32[2048,512]{1,0:T(8,128)}, u32[]{:S(2)}) %copy-start) | copy-done | bytes 4194328
  13.7 0.6 %near.1.cross_in_ref = f32[128,512]{1,0:T(8,128)S(1)} custom-call(bf16[512,256]{1,0:T(8,128)(2,1)S(1)} %get-tuple-element.22.own_ref.refs_0_, bf16[512,256]{1,0:T(8,128)(2,1)S(1)} %get-tuple-element.23.mate_ref.refs_1_, f32[2048,512]{1,0:T(8,128)S(1)} %copy-done), custom_call_target="tpu_custom_call" | custom-call | tf_op jit(solution)/shard_map/near/pallas_call | solution.py:250
  14.4 0.5 far.1
  14.9 0.0 collective-permute-done.9.piece_ref
  14.9 0.5 %last.1 = (bf16[512,256]{1,0:T(8,128)(2,1)S(1)}, f32[128,128]{1,0:T(8,128)S(1)}, f32[128,128]{1,0:T(8,128)S(1)}, f32[128,128]{1,0:T(8,128)S(1)}, f32[128,128]{1,0:T(8,128)S(1)}) custom-call(f32[512,128]{1,0:T(8,128)S(1)} %collective-permute-done.9.piece_ref, f32[2048,512]{1,0:T(8,128)S(1)} %copy-done, f32[128,512]{1,0:T(8,128)S(1)} %get-tuple-element.25.cross_in_ref), custom_call_target="tpu_custom_call" | custom-call | tf_op jit(solution)/shard_map/last/pallas_call | solution.py:263
  15.4 1.8 %collective-permute-start.10 = (f32[128,128]{1,0:T(8,128)S(1)}, f32[128,128]{1,0:T(8,128)S(1)}, u32[]{:S(2)}, u32[]{:S(2)}) collective-permute-start(f32[128,128]{1,0:T(8,128)S(1)} %get-tuple-element.28), channel_id=1, source_target_pairs={{0,4},{4,0},{8,12},{12,8},{16,20},{20,16},{24,28},{28,24},{1,5},{5... | collective-permute-start | bytes 196616 | tf_op jit(solution)/shard_map/ppermute | solution.py:207
  17.2 1.6 %collective-permute-start.11 = (f32[128,128]{1,0:T(8,128)S(1)}, f32[128,128]{1,0:T(8,128)S(1)}, u32[]{:S(2)}, u32[]{:S(2)}) collective-permute-start(f32[128,128]{1,0:T(8,128)S(1)} %get-tuple-element.29), channel_id=1, source_target_pairs={{0,8},{4,12},{8,0},{12,4},{16,24},{20,28},{24,16},{28,20},{1,9},{5... | collective-permute-start | bytes 196616 | tf_op jit(solution)/shard_map/ppermute | solution.py:207
  18.8 0.1 collective-permute-start.12
  19.0 2.8 %collective-permute-start.3 = (f32[64,128]{1,0:T(8,128)S(1)}, f32[64,128]{1,0:T(8,128)S(1)}, u32[]{:S(2)}, u32[]{:S(2)}) collective-permute-start(f32[64,128]{1,0:T(8,128)S(1)} %get-tuple-element.19), channel_id=1, source_target_pairs={{0,12},{4,8},{8,4},{12,0},{16,28},{20,24},{24,20},{28,16},{1,13},{... | collective-permute-start | bytes 98312 | tf_op jit(solution)/shard_map/ppermute | solution.py:207
  21.8 0.4 collective-permute-start.2
  22.2 0.0 collective-permute-done.10
  22.2 0.3 collective-permute-start.1
  22.5 1.9 %collective-permute-done.12 = f32[128,128]{1,0:T(8,128)S(1)} collective-permute-done((f32[128,128]{1,0:T(8,128)S(1)}, f32[128,128]{1,0:T(8,128)S(1)}, u32[]{:S(2)}, u32[]{:S(2)}) %collective-permute-start.12) | collective-permute-done | bytes 65568 | tf_op jit(solution)/shard_map/ppermute | solution.py:207
  24.4 2.6 %collective-permute-start.13 = (f32[128,128]{1,0:T(8,128)S(1)}, f32[128,128]{1,0:T(8,128)S(1)}, u32[]{:S(2)}, u32[]{:S(2)}) collective-permute-start(f32[128,128]{1,0:T(8,128)S(1)} %add_add_fusion), channel_id=1, source_target_pairs={{0,16},{4,20},{8,24},{12,28},{16,0},{20,4},{24,8},{28,12},{1,17},{... | collective-permute-start | bytes 196616 | tf_op jit(solution)/shard_map/ppermute | solution.py:207
  27.0 0.0 collective-permute-done.3
  27.0 0.0 collective-permute-done.2
  27.1 1.7 %collective-permute-start.4 = (f32[64,128]{1,0:T(8,128)S(1)}, f32[64,128]{1,0:T(8,128)S(1)}, u32[]{:S(2)}, u32[]{:S(2)}) collective-permute-start(f32[64,128]{1,0:T(8,128)S(1)} %add_add_fusion.1), channel_id=1, source_target_pairs={{0,16},{4,20},{8,24},{12,28},{16,0},{20,4},{24,8},{28,12},{1,17},{... | collective-permute-start | bytes 98312 | tf_op jit(solution)/shard_map/ppermute | solution.py:207
  28.8 3.5 %collective-permute-done.4 = f32[64,128]{1,0:T(8,128)S(1)} collective-permute-done((f32[64,128]{1,0:T(8,128)S(1)}, f32[64,128]{1,0:T(8,128)S(1)}, u32[]{:S(2)}, u32[]{:S(2)}) %collective-permute-start.4) | collective-permute-done | bytes 32800 | tf_op jit(solution)/shard_map/ppermute | solution.py:207
  32.3 0.0 collective-permute-done.13
  32.3 1.1 %collective-permute-start.16 = (f32[128,128]{1,0:T(8,128)S(1)}, f32[128,128]{1,0:T(8,128)S(1)}, u32[]{:S(2)}, u32[]{:S(2)}) collective-permute-start(f32[128,128]{1,0:T(8,128)S(1)} %add.31.refs_4_), channel_id=1, source_target_pairs={{0,12},{4,8},{8,4},{12,0},{16,28},{20,24},{24,20},{28,16},{1,13},{... | collective-permute-start | bytes 196616 | tf_op jit(solution)/shard_map/ppermute | solution.py:207
  33.5 0.6 %collective-permute-start.15 = (f32[128,128]{1,0:T(8,128)S(1)}, f32[128,128]{1,0:T(8,128)S(1)}, u32[]{:S(2)}, u32[]{:S(2)}) collective-permute-start(f32[128,128]{1,0:T(8,128)S(1)} %add.31.refs_4_), channel_id=1, source_target_pairs={{0,8},{4,12},{8,0},{12,4},{16,24},{20,28},{24,16},{28,20},{1,9},{5... | collective-permute-start | bytes 196616 | tf_op jit(solution)/shard_map/ppermute | solution.py:207
  34.0 1.9 %collective-permute-start.14 = (f32[128,128]{1,0:T(8,128)S(1)}, f32[128,128]{1,0:T(8,128)S(1)}, u32[]{:S(2)}, u32[]{:S(2)}) collective-permute-start(f32[128,128]{1,0:T(8,128)S(1)} %add.31.refs_4_), channel_id=1, source_target_pairs={{0,4},{4,0},{8,12},{12,8},{16,20},{20,16},{24,28},{28,24},{1,5},{5... | collective-permute-start | bytes 196616 | tf_op jit(solution)/shard_map/ppermute | solution.py:207
  35.9 1.5 %collective-permute-start.6 = (f32[64,128]{1,0:T(8,128)S(1)}, f32[64,128]{1,0:T(8,128)S(1)}, u32[]{:S(2)}, u32[]{:S(2)}) collective-permute-start(f32[64,128]{1,0:T(8,128)S(1)} %add.27.refs_0_), channel_id=1, source_target_pairs={{0,2},{1,3},{2,0},{3,1},{4,6},{5,7},{6,4},{7,5},{8,10},{9,11},{10,... | collective-permute-start | bytes 98312 | tf_op jit(solution)/shard_map/ppermute | solution.py:207
  37.4 2.5 %collective-permute-done.6.refs_2_ = f32[64,128]{1,0:T(8,128)S(1)} collective-permute-done((f32[64,128]{1,0:T(8,128)S(1)}, f32[64,128]{1,0:T(8,128)S(1)}, u32[]{:S(2)}, u32[]{:S(2)}) %collective-permute-start.6) | collective-permute-done | bytes 32800 | tf_op jit(solution)/shard_map/ppermute | solution.py:207
  40.0 3.9 %factor.1 = (f32[128,128]{1,0:T(8,128)}, bf16[256,256]{1,0:T(8,128)(2,1)S(1)}) custom-call(f32[64,128]{1,0:T(8,128)S(1)} %add.27.refs_0_, f32[64,128]{1,0:T(8,128)S(1)} %collective-permute-done.5.refs_1_, f32[64,128]{1,0:T(8,128)S(1)} %collective-permute-done.6.refs_2_, f32[64,128]{1,0:T(8,128)S(1)} %collective-permute-done.7.refs_3_), custom_call_target="tpu_custom_call" | custom-call | tf_op jit(solution)/shard_map/factor/pallas_call | solution.py:279
  43.8 2.7 %final.1 = (f32[128,512]{1,0:T(8,128)}, f32[2048,512]{1,0:T(8,128)}) custom-call(bf16[256,256]{1,0:T(8,128)(2,1)S(1)} %get-tuple-element.21.solve_ref, f32[2048,512]{1,0:T(8,128)S(1)} %copy-done, bf16[512,256]{1,0:T(8,128)(2,1)S(1)} %get-tuple-element.22.own_ref.refs_0_, bf16[512,256]{1,0:T(8,128)(2,1)S(1)} %get-tuple-element.23.mate_ref.refs_1_, ...), custom_call_target="tpu_custom_call" | custom-call | tf_op jit(solution)/shard_map/final/pallas_call | solution.py:292
  (15 shorter events, 0.1 us)
Async XLA Ops:
  0.6 9.5 %collective-permute-start.8 = (f32[512,128]{1,0:T(8,128)}, f32[512,128]{1,0:T(8,128)S(1)}, u32[]{:S(2)}, u32[]{:S(2)}) collective-permute-start(f32[512,128]{1,0:T(8,128)} %panel_ref.1), channel_id=1, source_target_pairs={{0,2},{1,3},{2,0},{3,1},{4,6},{5,7},{6,4},{7,5},{8,10},{9,11},{10,... | collective-permute-start | bytes 786440 | tf_op jit(solution)/shard_map/ppermute | solution.py:207
  3.7 7.9 %collective-permute-start = (f32[512,128]{1,0:T(8,128)}, f32[512,128]{1,0:T(8,128)S(1)}, u32[]{:S(2)}, u32[]{:S(2)}) collective-permute-start(f32[512,128]{1,0:T(8,128)} %panel_ref.1), channel_id=1, source_target_pairs={{0,1},{1,0},{2,3},{3,2},{4,5},{5,4},{6,7},{7,6},{8,9},{9,8},{10,11... | collective-permute-start | bytes 786440 | tf_op jit(solution)/shard_map/ppermute | solution.py:207
  10.2 4.7 %collective-permute-start.9 = (f32[512,128]{1,0:T(8,128)S(1)}, f32[512,128]{1,0:T(8,128)S(1)}, u32[]{:S(2)}, u32[]{:S(2)}) collective-permute-start(f32[512,128]{1,0:T(8,128)S(1)} %collective-permute-done.8.piece_ref), channel_id=1, source_target_pairs={{0,1},{1,0},{2,3},{3,2},{4,5},{5,4},{6,7},{7,6},{8,9},{9,8},{10,11... | collective-permute-start | bytes 786440 | tf_op jit(solution)/shard_map/ppermute | solution.py:207
  11.6 2.2 %copy-start = (f32[2048,512]{1,0:T(8,128)S(1)}, f32[2048,512]{1,0:T(8,128)}, u32[]{:S(2)}) copy-start(f32[2048,512]{1,0:T(8,128)} %held_ref.7) | copy-start | bytes 12582916
  15.4 6.8 %collective-permute-start.10 = (f32[128,128]{1,0:T(8,128)S(1)}, f32[128,128]{1,0:T(8,128)S(1)}, u32[]{:S(2)}, u32[]{:S(2)}) collective-permute-start(f32[128,128]{1,0:T(8,128)S(1)} %get-tuple-element.28), channel_id=1, source_target_pairs={{0,4},{4,0},{8,12},{12,8},{16,20},{20,16},{24,28},{28,24},{1,5},{5... | collective-permute-start | bytes 196616 | tf_op jit(solution)/shard_map/ppermute | solution.py:207
  17.2 5.2 %collective-permute-start.11 = (f32[128,128]{1,0:T(8,128)S(1)}, f32[128,128]{1,0:T(8,128)S(1)}, u32[]{:S(2)}, u32[]{:S(2)}) collective-permute-start(f32[128,128]{1,0:T(8,128)S(1)} %get-tuple-element.29), channel_id=1, source_target_pairs={{0,8},{4,12},{8,0},{12,4},{16,24},{20,28},{24,16},{28,20},{1,9},{5... | collective-permute-start | bytes 196616 | tf_op jit(solution)/shard_map/ppermute | solution.py:207
  18.8 5.5 %collective-permute-start.12 = (f32[128,128]{1,0:T(8,128)S(1)}, f32[128,128]{1,0:T(8,128)S(1)}, u32[]{:S(2)}, u32[]{:S(2)}) collective-permute-start(f32[128,128]{1,0:T(8,128)S(1)} %get-tuple-element.30), channel_id=1, source_target_pairs={{0,12},{4,8},{8,4},{12,0},{16,28},{20,24},{24,20},{28,16},{1,13},{... | collective-permute-start | bytes 196616 | tf_op jit(solution)/shard_map/ppermute | solution.py:207
  19.0 8.1 %collective-permute-start.3 = (f32[64,128]{1,0:T(8,128)S(1)}, f32[64,128]{1,0:T(8,128)S(1)}, u32[]{:S(2)}, u32[]{:S(2)}) collective-permute-start(f32[64,128]{1,0:T(8,128)S(1)} %get-tuple-element.19), channel_id=1, source_target_pairs={{0,12},{4,8},{8,4},{12,0},{16,28},{20,24},{24,20},{28,16},{1,13},{... | collective-permute-start | bytes 98312 | tf_op jit(solution)/shard_map/ppermute | solution.py:207
  21.8 5.3 %collective-permute-start.2 = (f32[64,128]{1,0:T(8,128)S(1)}, f32[64,128]{1,0:T(8,128)S(1)}, u32[]{:S(2)}, u32[]{:S(2)}) collective-permute-start(f32[64,128]{1,0:T(8,128)S(1)} %get-tuple-element.19), channel_id=1, source_target_pairs={{0,8},{4,12},{8,0},{12,4},{16,24},{20,28},{24,16},{28,20},{1,9},{5... | collective-permute-start | bytes 98312 | tf_op jit(solution)/shard_map/ppermute | solution.py:207
  22.2 4.9 %collective-permute-start.1 = (f32[64,128]{1,0:T(8,128)S(1)}, f32[64,128]{1,0:T(8,128)S(1)}, u32[]{:S(2)}, u32[]{:S(2)}) collective-permute-start(f32[64,128]{1,0:T(8,128)S(1)} %get-tuple-element.19), channel_id=1, source_target_pairs={{0,4},{4,0},{8,12},{12,8},{16,20},{20,16},{24,28},{28,24},{1,5},{5... | collective-permute-start | bytes 98312 | tf_op jit(solution)/shard_map/ppermute | solution.py:207
  24.4 7.9 %collective-permute-start.13 = (f32[128,128]{1,0:T(8,128)S(1)}, f32[128,128]{1,0:T(8,128)S(1)}, u32[]{:S(2)}, u32[]{:S(2)}) collective-permute-start(f32[128,128]{1,0:T(8,128)S(1)} %add_add_fusion), channel_id=1, source_target_pairs={{0,16},{4,20},{8,24},{12,28},{16,0},{20,4},{24,8},{28,12},{1,17},{... | collective-permute-start | bytes 196616 | tf_op jit(solution)/shard_map/ppermute | solution.py:207
  27.1 5.2 %collective-permute-start.4 = (f32[64,128]{1,0:T(8,128)S(1)}, f32[64,128]{1,0:T(8,128)S(1)}, u32[]{:S(2)}, u32[]{:S(2)}) collective-permute-start(f32[64,128]{1,0:T(8,128)S(1)} %add_add_fusion.1), channel_id=1, source_target_pairs={{0,16},{4,20},{8,24},{12,28},{16,0},{20,4},{24,8},{28,12},{1,17},{... | collective-permute-start | bytes 98312 | tf_op jit(solution)/shard_map/ppermute | solution.py:207
  32.3 5.1 %collective-permute-start.7 = (f32[64,128]{1,0:T(8,128)S(1)}, f32[64,128]{1,0:T(8,128)S(1)}, u32[]{:S(2)}, u32[]{:S(2)}) collective-permute-start(f32[64,128]{1,0:T(8,128)S(1)} %add.27.refs_0_), channel_id=1, source_target_pairs={{0,3},{1,2},{2,1},{3,0},{4,7},{5,6},{6,5},{7,4},{8,11},{9,10},{10,... | collective-permute-start | bytes 98312 | tf_op jit(solution)/shard_map/ppermute | solution.py:207
  32.3 11.5 %collective-permute-start.16 = (f32[128,128]{1,0:T(8,128)S(1)}, f32[128,128]{1,0:T(8,128)S(1)}, u32[]{:S(2)}, u32[]{:S(2)}) collective-permute-start(f32[128,128]{1,0:T(8,128)S(1)} %add.31.refs_4_), channel_id=1, source_target_pairs={{0,12},{4,8},{8,4},{12,0},{16,28},{20,24},{24,20},{28,16},{1,13},{... | collective-permute-start | bytes 196616 | tf_op jit(solution)/shard_map/ppermute | solution.py:207
  33.5 10.4 %collective-permute-start.15 = (f32[128,128]{1,0:T(8,128)S(1)}, f32[128,128]{1,0:T(8,128)S(1)}, u32[]{:S(2)}, u32[]{:S(2)}) collective-permute-start(f32[128,128]{1,0:T(8,128)S(1)} %add.31.refs_4_), channel_id=1, source_target_pairs={{0,8},{4,12},{8,0},{12,4},{16,24},{20,28},{24,16},{28,20},{1,9},{5... | collective-permute-start | bytes 196616 | tf_op jit(solution)/shard_map/ppermute | solution.py:207
  34.0 9.8 %collective-permute-start.14 = (f32[128,128]{1,0:T(8,128)S(1)}, f32[128,128]{1,0:T(8,128)S(1)}, u32[]{:S(2)}, u32[]{:S(2)}) collective-permute-start(f32[128,128]{1,0:T(8,128)S(1)} %add.31.refs_4_), channel_id=1, source_target_pairs={{0,4},{4,0},{8,12},{12,8},{16,20},{20,16},{24,28},{28,24},{1,5},{5... | collective-permute-start | bytes 196616 | tf_op jit(solution)/shard_map/ppermute | solution.py:207
  35.9 4.0 %collective-permute-start.6 = (f32[64,128]{1,0:T(8,128)S(1)}, f32[64,128]{1,0:T(8,128)S(1)}, u32[]{:S(2)}, u32[]{:S(2)}) collective-permute-start(f32[64,128]{1,0:T(8,128)S(1)} %add.27.refs_0_), channel_id=1, source_target_pairs={{0,2},{1,3},{2,0},{3,1},{4,6},{5,7},{6,4},{7,5},{8,10},{9,11},{10,... | collective-permute-start | bytes 98312 | tf_op jit(solution)/shard_map/ppermute | solution.py:207
  37.4 2.5 %collective-permute-start.5 = (f32[64,128]{1,0:T(8,128)S(1)}, f32[64,128]{1,0:T(8,128)S(1)}, u32[]{:S(2)}, u32[]{:S(2)}) collective-permute-start(f32[64,128]{1,0:T(8,128)S(1)} %add.27.refs_0_), channel_id=1, source_target_pairs={{0,1},{1,0},{2,3},{3,2},{4,5},{5,4},{6,7},{7,6},{8,9},{9,8},{10,11... | collective-permute-start | bytes 98312 | tf_op jit(solution)/shard_map/ppermute | solution.py:207
